TPU v7x, 32 devices: a whole 2x2x4 slice. The times are simulated.
32 devices in a mesh: dp: 4 (over z), expert: 8 (over y, x, core).
Axes of the slice: x: 2, y: 2, z: 4, core: 2. Of those that a mesh axis runs over, the one named last changes fastest.
Arguments:
- residual: bfloat16 [4096, 1280], P(('dp', 'expert')), may hold values from -6 to 6
- context: bfloat16 [4096, 1280], P(('dp', 'expert')), may hold values from -6 to 6
- w_out: bfloat16 [1280, 1280], P(('dp', 'expert')), may hold values from -0.15625 to 0.15625
- w_router: bfloat16 [1280, 16], replicated, may hold values from -0.15625 to 0.15625
- expert_ids: int32 [4096, 2], P(('dp', 'expert')), may hold values from 0 to 15, all different within a row; in each aligned block of 128 rows (0 to 127, 128 to 255, ...) at most 20 rows name the same one
- w_fc1: bfloat16 [16, 1280, 5120], P('expert', None, 'dp'), may hold values from -0.15625 to 0.15625
- w_fc2: bfloat16 [16, 5120, 1280], P('expert', 'dp'), may hold values from -0.078125 to 0.078125
- cotangent: bfloat16 [4096, 1280], P(('dp', 'expert')), may hold values from -6 to 6
Outputs:
- layer_out: bfloat16 [4096, 1280], P(('dp', 'expert'))
- d_residual: bfloat16 [4096, 1280], P(('dp', 'expert'))
- d_context: bfloat16 [4096, 1280], P(('dp', 'expert'))
- grad_out: float32 [1280, 1280], P(('dp', 'expert'))
- grad_router: float32 [1280, 16], P(('dp', 'expert'))
- grad_fc1: float32 [16, 1280, 5120], P('expert', None, 'dp')
- grad_fc2: float32 [16, 5120, 1280], P('expert', 'dp')
Inputs may be any that keep to these rules, and one draw needn't show every extreme that they name: `expert_ids`: each row names 2 different experts. Among the 128 rows of one device no expert is named more than 20 times, and some device has an expert named exactly 20 times.
All inputs are finite; a program needn't handle non-finite values.
Results may differ from a plain program's by a relative error of at most 0.01.
Values may be sent and summed in bfloat16 or wider, within the bound.
No kernel may reach another device: no remote copies, remote signals or barrier semaphores. Data moves between devices by JAX's collectives and lax.ppermute only.
A program may use at most 192 MiB of HBM per device.

v0:
```python
import functools

import jax
import jax.numpy as jnp
from jax import lax
from jax.experimental import pallas as pl
from jax.experimental.pallas import tpu as pltpu
from jax.sharding import PartitionSpec as P

LN_EPS = 1e-06
BF = jnp.bfloat16
F32 = jnp.float32
HI = lax.Precision.HIGHEST


def dot32(a, b, dims=((1,), (0,)), precision=None):
    return lax.dot_general(
        a, b, (dims, ((), ())), preferred_element_type=F32, precision=precision
    )


def swap(value, axis, bit):
    n = lax.axis_size(axis)
    return lax.ppermute(value, axis, [(i, i ^ bit) for i in range(n)])


def exchange(value):
    return lax.all_to_all(value, "expert", split_axis=0, concat_axis=0, tiled=True)


def chunk_of(size, most):
    for chunk in range(most - most % 128, 0, -128):
        if size % chunk == 0:
            return chunk
    return size


def flat(ref):
    return ref[...].reshape(-1, ref.shape[-1])


def row_block(a, size, step):
    if a.ndim == 3:
        return pl.BlockSpec((None, a.shape[1], size), lambda i, j: (i, 0, j * step))
    return pl.BlockSpec((a.shape[0], None, a.shape[2], size), lambda i, j: (0, i, 0, j * step))


def ffn_kernel(part, x_ref, c_ref, sel_ref, wr_ref, w1_ref, w2_ref, out_ref, back_ref, gh_ref, dp_ref, s_ref, acc_o, acc_b):
    x = flat(x_ref)
    c = flat(c_ref)
    g = jax.nn.sigmoid(jnp.sum(dot32(x, wr_ref[...]) * sel_ref[...], axis=1, keepdims=True))
    count = w1_ref.shape[1] // part
    across = ((1,), (1,))
    acc_o[...] = jnp.zeros_like(acc_o)
    acc_b[...] = jnp.zeros_like(acc_b)

    def body(i, score):
        span = pl.ds(pl.multiple_of(i * part, part), part)
        pre = dot32(x, w1_ref[:, span])
        dh = dot32(c, w2_ref[span, :], across) * g
        cdf = 0.5 * (1.0 + lax.erf(pre * 0.7071067811865476))
        hid = pre * cdf
        slope = cdf + pre * jnp.exp(-0.5 * pre * pre) * 0.3989422804014327
        dp = (dh * slope).astype(BF)
        gh_ref[:, span] = (hid * g).astype(BF)
        dp_ref[:, span] = dp
        acc_o[...] += dot32(hid.astype(BF), w2_ref[span, :])
        acc_b[...] += dot32(dp, w1_ref[:, span], across)
        return score + jnp.sum(dh * hid, axis=1, keepdims=True)

    score = lax.fori_loop(0, count, body, jnp.zeros_like(g))
    out_ref[...] = (acc_o[...] * g).astype(BF).reshape(out_ref.shape)
    back_ref[...] = acc_b[...].astype(BF).reshape(back_ref.shape)
    s_ref[...] = score


def ffn(x, c, sel, w_router, w1, w2):
    e, width, hidden = w1.shape
    rows = x.size // (e * width)
    experts = w_router.shape[1]
    row_spec = row_block(x, width, 0)

    def own(*shape):
        return pl.BlockSpec((None, *shape), lambda i, j: (i, 0, 0))

    return pl.pallas_call(
        functools.partial(ffn_kernel, chunk_of(hidden, 256)),
        grid=(e, 1),
        in_specs=[
            row_spec,
            row_spec,
            own(rows, experts),
            pl.BlockSpec((width, experts), lambda i, j: (0, 0)),
            own(width, hidden),
            own(hidden, width),
        ],
        out_specs=[row_spec, row_spec, own(rows, hidden), own(rows, hidden), own(rows, 1)],
        out_shape=[
            jax.ShapeDtypeStruct(x.shape, BF),
            jax.ShapeDtypeStruct(x.shape, BF),
            jax.ShapeDtypeStruct((e, rows, hidden), BF),
            jax.ShapeDtypeStruct((e, rows, hidden), BF),
            jax.ShapeDtypeStruct((e, rows, 1), F32),
        ],
        scratch_shapes=[pltpu.VMEM((rows, width), F32), pltpu.VMEM((rows, width), F32)],
        cost_estimate=pl.CostEstimate(
            flops=8 * e * rows * width * hidden,
            bytes_accessed=4 * e * width * hidden + 8 * e * rows * (width + hidden),
            transcendentals=2 * e * rows * hidden,
        ),
        compiler_params=pltpu.CompilerParams(dimension_semantics=("arbitrary", "arbitrary")),
    )(x, c, sel, w_router, w1, w2)


def wgrad_kernel(scale, pairs, *refs):
    left = jnp.concatenate([flat(r) for r in refs[:pairs]], axis=0)
    right = jnp.concatenate([flat(r) for r in refs[pairs:-1]], axis=0)
    refs[-1][0] = dot32(left, right, ((0,), (0,))) * scale


def wgrad(scale, e, lefts, rights):
    m = lefts[0].shape[-1]
    n = rights[0].shape[-1]
    mc = chunk_of(m, 640)
    rows = sum([a.size // (e * m) for a in lefts])
    return pl.pallas_call(
        functools.partial(wgrad_kernel, scale, len(lefts)),
        grid=(e, m // mc),
        in_specs=[row_block(a, mc, 1) for a in lefts] + [row_block(b, n, 0) for b in rights],
        out_specs=pl.BlockSpec((1, mc, n), lambda i, j: (i, j, 0)),
        out_shape=jax.ShapeDtypeStruct((e, m, n), F32),
        cost_estimate=pl.CostEstimate(
            flops=2 * e * rows * m * n,
            bytes_accessed=4 * e * m * n + 2 * e * rows * (m + n),
            transcendentals=0,
        ),
        compiler_params=pltpu.CompilerParams(dimension_semantics=("arbitrary", "arbitrary")),
    )(*lefts, *rights)


def on_device(residual, context, w_out, w_router, expert_ids, w_fc1, w_fc2, cotangent):
    tok, width = residual.shape
    top_k = expert_ids.shape[1]
    n_dp = lax.axis_size("dp")
    n_ex = lax.axis_size("expert")
    z = lax.axis_index("dp")
    ex = lax.axis_index("expert")
    exp_dev = w_fc1.shape[0]
    experts = exp_dev * n_ex
    cap = max(2, (5 * top_k * tok + 4 * experts - 1) // (4 * experts))
    scale = float(tok * n_dp * n_ex) ** (-0.5)
    shard = w_out.shape[0]
    rows_q = n_dp * shard
    hi, lo = n_ex // 2, n_ex // 4
    groups = [list(range(n_dp // 2)), list(range(n_dp // 2, n_dp))]
    per = n_dp // 2
    seg = per * cap
    slots = n_ex * exp_dev * seg

    own_ids = expert_ids.T
    ids = [own_ids] + [swap(own_ids, "dp", j) for j in range(1, n_dp)]

    col = lax.broadcasted_iota(jnp.int32, (1, width), 1)
    place = col // rows_q
    within = col % rows_q
    rel = jnp.zeros_like(place)
    b, m = 1, n_ex // 2
    while m:
        rel = rel + ((place // m) % 2) * b
        b, m = b * 2, m // 2
    source = ((z ^ (within // shard)) * n_ex + (ex ^ rel)) * shard + within % shard
    reorder = (lax.broadcasted_iota(jnp.int32, (width, width), 0) == source).astype(BF)
    ctx_rel = dot32(context, reorder).astype(BF)

    tri = (
        lax.broadcasted_iota(jnp.int32, (tok, tok), 0)
        < lax.broadcasted_iota(jnp.int32, (tok, tok), 1)
    ).astype(BF)
    e_iota = lax.broadcasted_iota(jnp.int32, (experts, tok), 0)

    def spots_of(block):
        hot = [(e_iota == block[k : k + 1]).astype(F32) for k in range(top_k)]
        before = dot32(sum(hot).astype(BF), tri)
        return [jnp.sum(h * before, axis=0, keepdims=True).astype(jnp.int32) for h in hot]

    own_spots = spots_of(own_ids)
    spot_iota = lax.broadcasted_iota(jnp.int32, (experts * cap, 1), 0)
    own_map = sum([(spot_iota == own_ids[k : k + 1] * cap + own_spots[k]).astype(BF) for k in range(top_k)])
    own_sent = dot32(own_map, cotangent).astype(BF)
    own_cot = exchange(own_sent)

    ids = lax.optimization_barrier(ids)
    spots = [spots_of(block) for block in ids]
    slot_iota = lax.broadcasted_iota(jnp.int32, (slots, 1), 0)
    maps = []
    for group in groups:
        by_k = []
        for k in range(top_k):
            target = [
                (ids[j][k : k + 1] // exp_dev) * (exp_dev * seg)
                + (ids[j][k : k + 1] % exp_dev) * seg
                + i * cap
                + spots[j][k]
                for i, j in enumerate(group)
            ]
            by_k.append((slot_iota == jnp.concatenate(target, axis=1)).astype(BF))
        maps.append(by_k)
    merged = [m[0] + m[1] for m in maps]

    def spread(value):
        n = value.shape[1]
        padded = -(-n // 1024) * 1024
        tile = jnp.pad(value, ((0, 0), (0, padded - n))).reshape(-1, 128)
        got = exchange(tile)
        return got.reshape(n_ex, padded)[:, :n]

    others = []
    for group, by_k in zip(groups, maps):
        total = None
        for k in range(top_k):
            value = jnp.concatenate([ids[j][1 - k : 2 - k] for j in group], axis=1).astype(BF)
            term = dot32(value, by_k[k], ((1,), (1,)))
            total = term if total is None else total + term
        others.append(total.reshape(n_ex, exp_dev * seg))
    others = spread(jnp.concatenate(others, axis=1))
    rows = n_ex * seg
    sels = []
    own_expert = ex * exp_dev + lax.broadcasted_iota(jnp.int32, (exp_dev, 1, 1), 0)
    lane_expert = lax.broadcasted_iota(jnp.int32, (1, 1, experts), 2)
    for g in range(len(groups)):
        other = others[:, g * exp_dev * seg : (g + 1) * exp_dev * seg]
        if g == 0:
            other = other.reshape(n_ex, exp_dev, per, cap).transpose(1, 2, 0, 3)
        else:
            other = other.reshape(n_ex, exp_dev, seg).transpose(1, 0, 2)
        other = other.reshape(exp_dev, rows, 1)
        sels.append(
            (lane_expert == own_expert).astype(F32)
            - (lane_expert == other.astype(jnp.int32)).astype(F32)
        )

    def dispatch(blocks, hot):
        sent = dot32(hot, jnp.concatenate(blocks, axis=0)).astype(BF)
        return exchange(sent).reshape(n_ex, exp_dev, seg, width)

    near, far = groups
    line = exp_dev * rows
    at = lax.broadcasted_iota(jnp.int32, (line, 1), 0)
    e_at, blk_at, src_at, pos_at = at // rows, at % rows // (n_ex * cap), at % (n_ex * cap) // cap, at % cap
    came_from = ((blk_at * n_ex + src_at) * exp_dev + e_at) * cap + pos_at
    arrange = (came_from == lax.broadcasted_iota(jnp.int32, (line, line), 1)).astype(BF)

    def gather_near(own):
        every = [own] + [swap(own, "dp", j) for j in near[1:]]
        return dot32(arrange, jnp.concatenate(every, axis=0)).astype(BF).reshape(exp_dev, rows, width)

    cot_near = gather_near(own_cot)
    cots = [swap(cotangent, "dp", j) for j in far]
    slot_cot = [cot_near, dispatch(cots, merged[1])]

    w_dp = jnp.concatenate([w_out] + [swap(w_out, "dp", j) for j in range(1, n_dp)], axis=0)
    from_hi = swap(w_dp, "expert", hi)
    from_lo = swap(w_dp, "expert", lo)
    half_q = rows_q // 2
    diag_a = swap(from_hi[:half_q], "expert", lo)
    diag_b = swap(from_lo[half_q:], "expert", hi)
    w_rel = [jnp.concatenate([w_dp, from_hi, from_lo, diag_a, diag_b], axis=0)]
    bit = lo // 2
    while bit:
        w_rel = w_rel + [swap(piece, "expert", bit) for piece in w_rel]
        bit //= 2

    stream = residual.astype(F32)
    span = w_rel[0].shape[0]
    for i, piece in enumerate(w_rel):
        stream = stream + dot32(ctx_rel[:, i * span : (i + 1) * span], piece)
    average = jnp.mean(stream, axis=1, keepdims=True)
    centred = stream - average
    variance = jnp.mean(centred * centred, axis=1, keepdims=True)
    inv_std = lax.rsqrt(variance + LN_EPS)
    normed = centred * inv_std
    normed_bf = normed.astype(BF)
    xs = [swap(normed_bf, "dp", j) for j in far]
    own_in = exchange(dot32(own_map, normed_bf).astype(BF))
    slot_in = [gather_near(own_in), dispatch(xs, merged[1])]

    normed_rel = dot32(normed_bf, reorder).astype(BF)
    logits = dot32(w_router, normed_bf, ((0,), (1,)))
    late_ids = lax.optimization_barrier(own_ids)
    picks = [(e_iota == late_ids[k : k + 1]).astype(F32) for k in range(top_k)]
    chosen = jnp.concatenate([jnp.sum(h * logits, axis=0, keepdims=True) for h in picks], axis=0)
    gates = jax.nn.sigmoid(chosen - chosen[::-1])

    results = []
    for x, c, sel in zip(slot_in, slot_cot, sels):
        results.append(ffn(x, c, sel, w_router, w_fc1, w_fc2))

    def collect(near_part, far_part):
        pieces = dot32(arrange, near_part.reshape(line, width), ((0,), (0,))).astype(BF)
        size = line // per
        slots_own = pieces[:size].astype(F32)
        for j in near[1:]:
            slots_own = slots_own + swap(pieces[j * size : (j + 1) * size], "dp", j).astype(F32)
        got = exchange(slots_own.astype(BF))
        total = dot32(own_map, got, ((0,), (0,)))
        got = exchange(far_part.reshape(-1, width))
        parts = dot32(merged[1], got, ((0,), (0,))).astype(BF)
        for i, j in enumerate(far):
            total = total + swap(parts[i * tok : (i + 1) * tok], "dp", j).astype(F32)
        return total

    back_sum = collect(results[0][1], results[1][1])
    score = [
        results[0][4].reshape(exp_dev, per, n_ex, cap).transpose(2, 0, 1, 3).reshape(n_ex, exp_dev * seg),
        results[1][4].reshape(exp_dev, n_ex, seg).transpose(1, 0, 2).reshape(n_ex, exp_dev * seg),
    ]
    score = spread(jnp.concatenate(score, axis=1))
    part = exp_dev * seg
    score_parts = []
    for g, by_k in enumerate(maps):
        packed = score[:, g * part : (g + 1) * part].reshape(1, slots)
        both = jnp.concatenate([dot32(packed, by_k[k].astype(F32), precision=HI) for k in range(top_k)], axis=0)
        score_parts += [both[:, i * tok : (i + 1) * tok] for i in range(per)]
    score_sum = score_parts[0]
    for j in range(1, n_dp):
        score_sum = score_sum + swap(score_parts[j], "dp", j)
    mixture = collect(results[0][0], results[1][0])
    d_chosen = score_sum - gates * jnp.sum(score_sum, axis=0, keepdims=True)
    d_logits = sum([picks[k] * d_chosen[k : k + 1] for k in range(top_k)])
    d_normed = back_sum + dot32(d_logits, w_router.astype(F32), ((0,), (1,)), precision=HI)
    cot_float = cotangent.astype(F32)
    d_stream = cot_float + inv_std * (
        d_normed
        - jnp.mean(d_normed, axis=1, keepdims=True)
        - normed * jnp.mean(d_normed * normed, axis=1, keepdims=True)
    )
    d_residual, late_stream = lax.optimization_barrier((d_stream.astype(BF), stream))
    layer_out = (late_stream + mixture).astype(BF)
    d_rel = jnp.concatenate([dot32(d_residual, piece, ((1,), (1,))).astype(BF) for piece in w_rel], axis=1)
    d_context = dot32(d_rel, reorder, ((1,), (1,))).astype(BF)

    rest, thirds = d_logits, []
    for _ in range(3):
        thirds.append(rest.astype(BF))
        rest = rest - thirds[-1].astype(F32)
    thirds = jnp.concatenate(thirds, axis=0)
    thirds = jnp.pad(thirds, ((0, -thirds.shape[0] % 128), (0, 0)))

    def sums_of(cols):
        return [
            dot32(ctx_rel[:, cols], d_residual, ((0,), (0,))),
            dot32(normed_rel[:, cols], thirds, ((0,), (1,))),
        ]

    half = width // 2
    sent = jnp.concatenate([v.astype(BF) for v in sums_of(slice(half, width))], axis=1)
    got = swap(sent, "expert", 1).astype(F32)
    part_out, part_router = sums_of(slice(0, half))
    part_out, part_router = part_out + got[:, :width], part_router + got[:, width:]
    bit = 2
    while bit < lo:
        half = half // 2
        sent = jnp.concatenate([part_out[half:], part_router[half:]], axis=1).astype(BF)
        got = swap(sent, "expert", bit).astype(F32)
        part_out, part_router = part_out[:half] + got[:, :width], part_router[:half] + got[:, width:]
        bit *= 2
    mid = width // 2
    left = [part_out[i * rows_q : (i + 1) * rows_q, :mid] for i in range(4)]
    right = [
        jnp.concatenate([part_out[i * rows_q : (i + 1) * rows_q, mid:], part_router[i * rows_q : (i + 1) * rows_q]], axis=1)
        for i in range(4)
    ]
    got_l = swap(jnp.concatenate([left[2], left[3]], axis=0).astype(BF), "expert", lo).astype(F32)
    got_r = swap(jnp.concatenate([right[1], right[3]], axis=0).astype(BF), "expert", hi).astype(F32)
    fin_l = swap((left[1] + got_l[rows_q:]).astype(BF), "expert", hi).astype(F32)
    fin_r = swap((right[2] + got_r[rows_q:]).astype(BF), "expert", lo).astype(F32)
    kept = jnp.concatenate([left[0] + got_l[:rows_q] + fin_l, right[0] + got_r[:rows_q] + fin_r], axis=1)
    grads = kept[:shard]
    for j in range(1, n_dp):
        grads = grads + swap(kept[j * shard : (j + 1) * shard].astype(BF), "dp", j).astype(F32)
    grads = scale * grads
    grad_out = grads[:, :width]
    grad_router = sum([grads[:, width + i * experts : width + (i + 1) * experts] for i in range(3)])

    grad_fc1 = wgrad(scale, exp_dev, slot_in, [r[3] for r in results])
    grad_fc2 = wgrad(scale, exp_dev, [r[2] for r in results], slot_cot)
    return (layer_out, d_residual, d_context, grad_out, grad_router, grad_fc1, grad_fc2)


def solution(mesh):
    rows = P(("dp", "expert"), None)
    first = P("expert", None, "dp")
    second = P("expert", "dp", None)

    return jax.shard_map(
        on_device,
        mesh=mesh,
        in_specs=(rows, rows, rows, P(), rows, first, second, rows),
        out_specs=(rows, rows, rows, rows, rows, first, second),
        check_vma=False,
    )
```

profile of v0, /device:TPU:0, one launch (start us, length us, event | category | flops | bytes accessed | tf_op | source)
XLA Modules:
  0.0 379.8 jit_solution(18319009101871140071)
XLA Ops:
  0.6 5.1 %collective-permute-start.12 = (s32[2,128]{1,0:T(2,128)}, s32[2,128]{1,0:T(2,128)S(1)}, u32[]{:S(2)}, u32[]{:S(2)}) collective-permute-start(s32[2,128]{1,0:T(2,128)} %bitcast.177), channel_id=1, source_target_pairs={{0,24},{8,16},{16,8},{24,0},{1,25},{9,17},{17,9},{25,1},{2,26},{10... | collective-permute-start | bytes 3080 | tf_op jit(solution)/shard_map/ppermute | solution.py:24
  6.4 2.3 collective-permute-start.1
  15.0 3.7 collective-permute-start.17
  19.2 3.3 collective-permute-done.2
  26.5 5.5 %collective-permute-done.4 = bf16[160,1280]{1,0:T(8,128)(2,1)S(1)} collective-permute-done((bf16[160,1280]{1,0:T(8,128)(2,1)}, bf16[160,1280]{1,0:T(8,128)(2,1)S(1)}, u32[]{:S(2)}, u32[]{:S(2)}) %collective-permute-start.4) | collective-permute-done | bytes 409632 | tf_op jit(solution)/shard_map/ppermute | solution.py:24
  36.3 4.8 %collective-permute-done.5 = bf16[80,1280]{1,0:T(8,128)(2,1)S(1)} collective-permute-done((bf16[80,1280]{1,0:T(8,128)(2,1)S(1)}, bf16[80,1280]{1,0:T(8,128)(2,1)S(1)}, u32[]{:S(2)}, u32[]{:S(2)}) %collective-permute-start.5) | collective-permute-done | bytes 204832 | tf_op jit(solution)/shard_map/ppermute | solution.py:24
  43.6 3.3 all-to-all-start.2
  51.8 4.2 %all-to-all-start.1 = ((bf16[8,40,1280]{2,1,0:T(8,128)(2,1)}), bf16[8,40,1280]{2,1,0:T(8,128)(2,1)}, u32[]{:S(2)}, u32[]{:S(2)}) async-start(bf16[8,40,1280]{2,1,0:T(8,128)(2,1)} %bitcast.11), calls=%async_computation.1 | async-start | bytes 1638400 | tf_op jit(solution)/shard_map/all_to_all | solution.py:28
  57.4 11.5 %all-to-all-done.1 = bf16[8,40,1280]{2,1,0:T(8,128)(2,1)} async-done(((bf16[8,40,1280]{2,1,0:T(8,128)(2,1)}), bf16[8,40,1280]{2,1,0:T(8,128)(2,1)}, u32[]{:S(2)}, u32[]{:S(2)}) %all-to-all-start.1) | async-done | bytes 819232 | tf_op jit(solution)/shard_map/all_to_all | solution.py:28
  68.9 4.2 %all-to-all-start = ((bf16[8,40,1280]{2,1,0:T(8,128)(2,1)}), bf16[8,40,1280]{2,1,0:T(8,128)(2,1)}, u32[]{:S(2)}, u32[]{:S(2)}) async-start(bf16[8,40,1280]{2,1,0:T(8,128)(2,1)} %bitcast.8), calls=%async_computation | async-start | bytes 1638400 | tf_op jit(solution)/shard_map/all_to_all | solution.py:28
  74.1 12.2 %collective-permute-start.9 = (bf16[320,1280]{1,0:T(8,128)(2,1)}, bf16[320,1280]{1,0:T(8,128)(2,1)}, u32[]{:S(2)}, u32[]{:S(2)}) collective-permute-start(bf16[320,1280]{1,0:T(8,128)(2,1)} %bitcast.12), channel_id=1, source_target_pairs={{0,8},{8,0},{16,24},{24,16},{1,9},{9,1},{17,25},{25,17},{2,10},{10... | collective-permute-start | bytes 2457608 | tf_op jit(solution)/shard_map/ppermute | solution.py:24
  86.4 2.9 convolution_convert_fusion.1
  89.3 4.3 %all-to-all-start.5 = ((bf16[8,80,1280]{2,1,0:T(8,128)(2,1)}), bf16[8,80,1280]{2,1,0:T(8,128)(2,1)}, u32[]{:S(2)}, u32[]{:S(2)}) async-start(bf16[8,80,1280]{2,1,0:T(8,128)(2,1)} %bitcast.167), calls=%async_computation.5 | async-start | bytes 3276800 | tf_op jit(solution)/shard_map/all_to_all | solution.py:28
  95.1 9.1 %collective-permute-start.8 = (bf16[320,1280]{1,0:T(8,128)(2,1)}, bf16[320,1280]{1,0:T(8,128)(2,1)}, u32[]{:S(2)}, u32[]{:S(2)}) collective-permute-start(bf16[320,1280]{1,0:T(8,128)(2,1)} %bitcast.9), channel_id=1, source_target_pairs={{0,8},{8,0},{16,24},{24,16},{1,9},{9,1},{17,25},{25,17},{2,10},{10... | collective-permute-start | bytes 2457608 | tf_op jit(solution)/shard_map/ppermute | solution.py:24
  105.5 4.1 %convolution_convert_fusion.5 = bf16[640,1280]{1,0:T(8,128)(2,1)} fusion(bf16[320,1280]{1,0:T(8,128)(2,1)} %collective-permute-done.9, bf16[320,1280]{1,0:T(8,128)(2,1)} %bitcast.12, s32[640]{0:T(1024)S(1)} %fusion.161), kind=kOutput, calls=%fused_computation.14 | convolution fusion | flops 1053081600 | bytes 3279360 | tf_op jit(solution)/shard_map/dot_general | solution.py:17
  110.0 2.8 collective-permute-start.14
  113.0 2.2 fusion.13
  115.2 15.9 %collective-permute-done.15 = bf16[128,1280]{1,0:T(8,128)(2,1)S(1)} collective-permute-done((bf16[128,1280]{1,0:T(8,128)(2,1)S(1)}, bf16[128,1280]{1,0:T(8,128)(2,1)S(1)}, u32[]{:S(2)}, u32[]{:S(2)}) %collective-permute-start.15) | collective-permute-done | bytes 327712 | tf_op jit(solution)/shard_map/ppermute | solution.py:24
  131.1 9.9 %collective-permute-done.14 = bf16[128,1280]{1,0:T(8,128)(2,1)S(1)} collective-permute-done((bf16[128,1280]{1,0:T(8,128)(2,1)S(1)}, bf16[128,1280]{1,0:T(8,128)(2,1)S(1)}, u32[]{:S(2)}, u32[]{:S(2)}) %collective-permute-start.14) | collective-permute-done | bytes 327712 | tf_op jit(solution)/shard_map/ppermute | solution.py:24
  142.8 4.5 %all-to-all-start.4 = ((bf16[8,80,1280]{2,1,0:T(8,128)(2,1)}), bf16[8,80,1280]{2,1,0:T(8,128)(2,1)}, u32[]{:S(2)}, u32[]{:S(2)}) async-start(bf16[8,80,1280]{2,1,0:T(8,128)(2,1)} %bitcast.168), calls=%async_computation.4 | async-start | bytes 3276800 | tf_op jit(solution)/shard_map/all_to_all | solution.py:28
  147.9 4.1 %convolution_convert_fusion.6 = bf16[640,1280]{1,0:T(8,128)(2,1)} fusion(bf16[320,1280]{1,0:T(8,128)(2,1)} %collective-permute-done.8, bf16[320,1280]{1,0:T(8,128)(2,1)} %bitcast.9, s32[640]{0:T(1024)S(1)} %fusion.161), kind=kOutput, calls=%fused_computation.15 | convolution fusion | flops 1053081600 | bytes 3279360 | tf_op jit(solution)/shard_map/dot_general | solution.py:17
  152.0 20.8 %shard_map.135 = (bf16[2,320,1280]{2,1,0:T(8,128)(2,1)}, bf16[2,320,1280]{2,1,0:T(8,128)(2,1)}, bf16[2,320,1280]{2,1,0:T(8,128)(2,1)}, bf16[2,320,1280]{2,1,0:T(8,128)(2,1)}, f32[2,320,1]{2,1,0:T(8,128)}) custom-call(bf16[2,320,1280]{2,1,0:T(8,128)(2,1)} %bitcast.163, bf16[2,320,1280]{2,1,0:T(8,128)(2,1)} %bitcast.161, ...), custom_call_target="tpu_custom_call" | custom-call | flops 8388608000 | bytes 26214400 | tf_op jit(solution)/shard_map/pallas_call | solution.py:86
  174.1 4.1 %convolution_convert_fusion.4 = bf16[640,1280]{1,0:T(8,128)(2,1)} fusion(bf16[640,1280]{1,0:T(8,128)(2,1)} %bitcast.206, s32[640]{0:T(1024)S(1)} %fusion.161), kind=kOutput, calls=%fused_computation.13 | convolution fusion | flops 1049804800 | bytes 3279360 | tf_op jit(solution)/shard_map/dot_general | solution.py:17
  178.3 19.6 %shard_map.136 = (bf16[8,2,40,1280]{3,2,1,0:T(8,128)(2,1)}, bf16[8,2,40,1280]{3,2,1,0:T(8,128)(2,1)}, bf16[2,320,1280]{2,1,0:T(8,128)(2,1)}, bf16[2,320,1280]{2,1,0:T(8,128)(2,1)}, f32[2,320,1]{2,1,0:T(8,128)}) custom-call(bf16[8,2,40,1280]{3,2,1,0:T(8,128)(2,1)} %bitcast.39.x_ref.refs_1_, bf16[8,2,40,1280]{3,2,1,0:T(8,128)(2,1)} %bitcast.41.c_ref.refs_3_, ...), custom_call_target="tpu_custom_call" | custom-call | flops 8388608000 | bytes 26214400 | tf_op jit(solution)/shard_map/pallas_call | solution.py:86
  200.0 3.9 %all-to-all-start.7 = ((f32[8,8,128]{2,1,0:T(8,128)}), f32[8,8,128]{2,1,0:T(8,128)S(1)}, u32[]{:S(2)}, u32[]{:S(2)}) async-start(f32[8,8,128]{2,1,0:T(8,128)} %copy.39), calls=%async_computation.7 | async-start | bytes 65536 | tf_op jit(solution)/shard_map/all_to_all | solution.py:28
  203.9 3.0 convolution_convert_fusion.3
  212.8 4.3 %all-to-all-start.6 = ((bf16[8,80,1280]{2,1,0:T(8,128)(2,1)}), bf16[8,80,1280]{2,1,0:T(8,128)(2,1)}, u32[]{:S(2)}, u32[]{:S(2)}) async-start(bf16[8,80,1280]{2,1,0:T(8,128)(2,1)} %bitcast.166), calls=%async_computation.6 | async-start | bytes 3276800 | tf_op jit(solution)/shard_map/all_to_all | solution.py:28
  221.8 2.4 collective-permute-start.22
  225.3 11.4 %shard_map.137 = f32[2,1280,1280]{2,1,0:T(8,128)} custom-call(bf16[2,320,1280]{2,1,0:T(8,128)(2,1)} %bitcast.164, bf16[8,2,40,1280]{3,2,1,0:T(8,128)(2,1)} %bitcast.39.x_ref.refs_1_, bf16[2,320,1280]{2,1,0:T(8,128)(2,1)} %get-tuple-element.35.refs_2_, bf16[2,320,1280]{2,1,0:T(8,128)(2,1)} %get-tuple-element.36.refs_3_), custom_call_target="tpu_custom_call" | custom-call | flops 4194304000 | bytes 19660800 | tf_op jit(solution)/shard_map/pallas_call | solution.py:126
  236.7 10.4 %collective-permute-done.21 = f32[2,128]{1,0:T(2,128)S(1)} collective-permute-done((f32[2,128]{1,0:T(2,128)}, f32[2,128]{1,0:T(2,128)S(1)}, u32[]{:S(2)}, u32[]{:S(2)}) %collective-permute-start.21) | collective-permute-done | bytes 1056 | tf_op jit(solution)/shard_map/ppermute | solution.py:24
  249.4 2.3 add_convert_fusion.1
  251.7 3.8 %all-to-all-start.3 = ((bf16[8,40,1280]{2,1,0:T(8,128)(2,1)}), bf16[8,40,1280]{2,1,0:T(8,128)(2,1)S(1)}, u32[]{:S(2)}, u32[]{:S(2)}) async-start(bf16[8,40,1280]{2,1,0:T(8,128)(2,1)} %bitcast.160), calls=%async_computation.3 | async-start | bytes 1638400 | tf_op jit(solution)/shard_map/all_to_all | solution.py:28
  263.5 4.9 %all-to-all-done.3 = bf16[8,40,1280]{2,1,0:T(8,128)(2,1)S(1)} async-done(((bf16[8,40,1280]{2,1,0:T(8,128)(2,1)}), bf16[8,40,1280]{2,1,0:T(8,128)(2,1)S(1)}, u32[]{:S(2)}, u32[]{:S(2)}) %all-to-all-start.3) | async-done | bytes 819232 | tf_op jit(solution)/shard_map/all_to_all | solution.py:28
  268.4 4.3 %all-to-all-start.9 = ((bf16[8,80,1280]{2,1,0:T(8,128)(2,1)}), bf16[8,80,1280]{2,1,0:T(8,128)(2,1)}, u32[]{:S(2)}, u32[]{:S(2)}) async-start(bf16[8,80,1280]{2,1,0:T(8,128)(2,1)} %bitcast.165), calls=%async_computation.9 | async-start | bytes 3276800 | tf_op jit(solution)/shard_map/all_to_all | solution.py:28
  272.8 11.0 %collective-permute-done.18 = bf16[128,1280]{1,0:T(8,128)(2,1)} collective-permute-done((bf16[128,1280]{1,0:T(8,128)(2,1)}, bf16[128,1280]{1,0:T(8,128)(2,1)}, u32[]{:S(2)}, u32[]{:S(2)}) %collective-permute-start.18) | collective-permute-done | bytes 327712 | tf_op jit(solution)/shard_map/ppermute | solution.py:24
  288.7 2.3 add_convert_fusion
  290.9 3.5 all-to-all-done.9
  294.5 3.5 all-to-all-start.8
  301.1 5.1 %collective-permute-start.24 = (bf16[128,1280]{1,0:T(8,128)(2,1)}, bf16[128,1280]{1,0:T(8,128)(2,1)}, u32[]{:S(2)}, u32[]{:S(2)}) collective-permute-start(bf16[128,1280]{1,0:T(8,128)(2,1)} %get-tuple-element.88), channel_id=1, source_target_pairs={{0,16},{8,24},{16,0},{24,8},{1,17},{9,25},{17,1},{25,9},{2,18},{10... | collective-permute-start | bytes 983048 | tf_op jit(solution)/shard_map/ppermute | solution.py:24
  307.7 11.4 %shard_map.138 = f32[2,1280,1280]{2,1,0:T(8,128)} custom-call(bf16[2,320,1280]{2,1,0:T(8,128)(2,1)} %get-tuple-element.37.refs_0_, bf16[2,320,1280]{2,1,0:T(8,128)(2,1)} %get-tuple-element.38.refs_1_, bf16[2,320,1280]{2,1,0:T(8,128)(2,1)} %bitcast.162, bf16[8,2,40,1280]{3,2,1,0:T(8,128)(2,1)} %bitcast.41.c_ref.refs_3_), custom_call_target="tpu_custom_call" | custom-call | flops 4194304000 | bytes 19660800 | tf_op jit(solution)/shard_map/pallas_call | solution.py:126
  319.1 10.0 %collective-permute-done.24 = bf16[128,1280]{1,0:T(8,128)(2,1)} collective-permute-done((bf16[128,1280]{1,0:T(8,128)(2,1)}, bf16[128,1280]{1,0:T(8,128)(2,1)}, u32[]{:S(2)}, u32[]{:S(2)}) %collective-permute-start.24) | collective-permute-done | bytes 327712 | tf_op jit(solution)/shard_map/ppermute | solution.py:24
  338.4 6.9 %collective-permute-done.27 = bf16[320,640]{1,0:T(8,128)(2,1)S(1)} collective-permute-done((bf16[320,640]{1,0:T(8,128)(2,1)S(1)}, bf16[320,640]{1,0:T(8,128)(2,1)S(1)}, u32[]{:S(2)}, u32[]{:S(2)}) %collective-permute-start.27) | collective-permute-done | bytes 409632 | tf_op jit(solution)/shard_map/ppermute | solution.py:24
  346.7 2.6 collective-permute-done.29
  349.3 3.1 collective-permute-done.28
  355.6 3.9 %collective-permute-done.30 = bf16[160,768]{1,0:T(8,128)(2,1)S(1)} collective-permute-done((bf16[160,768]{1,0:T(8,128)(2,1)S(1)}, bf16[160,768]{1,0:T(8,128)(2,1)S(1)}, u32[]{:S(2)}, u32[]{:S(2)}) %collective-permute-start.30) | collective-permute-done | bytes 245792 | tf_op jit(solution)/shard_map/ppermute | solution.py:24
  359.7 7.8 %collective-permute-start.31 = (bf16[40,1408]{1,0:T(8,128)(2,1)S(1)}, bf16[40,1408]{1,0:T(8,128)(2,1)S(1)}, u32[]{:S(2)}, u32[]{:S(2)}) collective-permute-start(bf16[40,1408]{1,0:T(8,128)(2,1)S(1)} %get-tuple-element.92), channel_id=1, source_target_pairs={{0,8},{8,0},{16,24},{24,16},{1,9},{9,1},{17,25},{25,17},{2,10},{10... | collective-permute-start | bytes 337928 | tf_op jit(solution)/shard_map/ppermute | solution.py:24
  371.8 2.9 collective-permute-done.33
  374.7 3.6 collective-permute-done.32
  (237 shorter events, 85.4 us)
Async XLA Ops:
  0.6 14.2 %collective-permute-start.12 = (s32[2,128]{1,0:T(2,128)}, s32[2,128]{1,0:T(2,128)S(1)}, u32[]{:S(2)}, u32[]{:S(2)}) collective-permute-start(s32[2,128]{1,0:T(2,128)} %bitcast.177), channel_id=1, source_target_pairs={{0,24},{8,16},{16,8},{24,0},{1,25},{9,17},{17,9},{25,1},{2,26},{10... | collective-permute-start | bytes 3080 | tf_op jit(solution)/shard_map/ppermute | solution.py:24
  5.8 9.3 %collective-permute-start.11 = (s32[2,128]{1,0:T(2,128)}, s32[2,128]{1,0:T(2,128)S(1)}, u32[]{:S(2)}, u32[]{:S(2)}) collective-permute-start(s32[2,128]{1,0:T(2,128)} %bitcast.178), channel_id=1, source_target_pairs={{0,16},{8,24},{16,0},{24,8},{1,17},{9,25},{17,1},{25,9},{2,18},{10... | collective-permute-start | bytes 3080 | tf_op jit(solution)/shard_map/ppermute | solution.py:24
  5.8 13.0 %collective-permute-start.10 = (s32[2,128]{1,0:T(2,128)}, s32[2,128]{1,0:T(2,128)S(1)}, u32[]{:S(2)}, u32[]{:S(2)}) collective-permute-start(s32[2,128]{1,0:T(2,128)} %bitcast.179), channel_id=1, source_target_pairs={{0,8},{8,0},{16,24},{24,16},{1,9},{9,1},{17,25},{25,17},{2,10},{10... | collective-permute-start | bytes 3080 | tf_op jit(solution)/shard_map/ppermute | solution.py:24
  6.4 12.8 %collective-permute-start.1 = (bf16[40,1280]{1,0:T(8,128)(2,1)}, bf16[40,1280]{1,0:T(8,128)(2,1)S(1)}, u32[]{:S(2)}, u32[]{:S(2)}) collective-permute-start(bf16[40,1280]{1,0:T(8,128)(2,1)} %param.10), channel_id=1, source_target_pairs={{0,16},{8,24},{16,0},{24,8},{1,17},{9,25},{17,1},{25,9},{2,18},{10... | collective-permute-start | bytes 307208 | tf_op jit(solution)/shard_map/ppermute | solution.py:24
  8.7 10.5 %collective-permute-start = (bf16[40,1280]{1,0:T(8,128)(2,1)}, bf16[40,1280]{1,0:T(8,128)(2,1)S(1)}, u32[]{:S(2)}, u32[]{:S(2)}) collective-permute-start(bf16[40,1280]{1,0:T(8,128)(2,1)} %param.10), channel_id=1, source_target_pairs={{0,8},{8,0},{16,24},{24,16},{1,9},{9,1},{17,25},{25,17},{2,10},{10... | collective-permute-start | bytes 307208 | tf_op jit(solution)/shard_map/ppermute | solution.py:24
  13.6 272.4 %copy-start.6 = (bf16[128,1280]{0,1:T(8,128)(2,1)}, bf16[128,1280]{0,1:T(8,128)(2,1)S(1)}, u32[]{:S(2)}) copy-start(bf16[128,1280]{0,1:T(8,128)(2,1)S(1)} %fusion.14) | copy-start | bytes 983044
  14.9 7.7 %collective-permute-start.2 = (bf16[40,1280]{1,0:T(8,128)(2,1)S(1)}, bf16[40,1280]{1,0:T(8,128)(2,1)S(1)}, u32[]{:S(2)}, u32[]{:S(2)}) collective-permute-start(bf16[40,1280]{1,0:T(8,128)(2,1)S(1)} %copy-done.13), channel_id=1, source_target_pairs={{0,24},{8,16},{16,8},{24,0},{1,25},{9,17},{17,9},{25,1},{2,26},{10... | collective-permute-start | bytes 307208 | tf_op jit(solution)/shard_map/ppermute | solution.py:24
  15.0 71.3 %collective-permute-start.17 = (bf16[128,1280]{1,0:T(8,128)(2,1)S(1)}, bf16[128,1280]{1,0:T(8,128)(2,1)}, u32[]{:S(2)}, u32[]{:S(2)}) collective-permute-start(bf16[128,1280]{1,0:T(8,128)(2,1)S(1)} %copy-done.8), channel_id=1, source_target_pairs={{0,24},{8,16},{16,8},{24,0},{1,25},{9,17},{17,9},{25,1},{2,26},{10... | collective-permute-start | bytes 983048 | tf_op jit(solution)/shard_map/ppermute | solution.py:24
  18.8 67.6 %collective-permute-start.16 = (bf16[128,1280]{1,0:T(8,128)(2,1)S(1)}, bf16[128,1280]{1,0:T(8,128)(2,1)}, u32[]{:S(2)}, u32[]{:S(2)}) collective-permute-start(bf16[128,1280]{1,0:T(8,128)(2,1)S(1)} %copy-done.8), channel_id=1, source_target_pairs={{0,16},{8,24},{16,0},{24,8},{1,17},{9,25},{17,1},{25,9},{2,18},{10... | collective-permute-start | bytes 983048 | tf_op jit(solution)/shard_map/ppermute | solution.py:24
  23.3 8.7 %collective-permute-start.4 = (bf16[160,1280]{1,0:T(8,128)(2,1)}, bf16[160,1280]{1,0:T(8,128)(2,1)S(1)}, u32[]{:S(2)}, u32[]{:S(2)}) collective-permute-start(bf16[160,1280]{1,0:T(8,128)(2,1)} %copy-done.16), channel_id=1, source_target_pairs={{0,2},{1,3},{2,0},{3,1},{4,6},{5,7},{6,4},{7,5},{8,10},{9,11},{10,... | collective-permute-start | bytes 1228808 | tf_op jit(solution)/shard_map/ppermute | solution.py:24
  24.8 10.4 %collective-permute-start.3 = (bf16[160,1280]{1,0:T(8,128)(2,1)}, bf16[160,1280]{1,0:T(8,128)(2,1)S(1)}, u32[]{:S(2)}, u32[]{:S(2)}) collective-permute-start(bf16[160,1280]{1,0:T(8,128)(2,1)} %copy-done.16), channel_id=1, source_target_pairs={{0,4},{1,5},{2,6},{3,7},{4,0},{5,1},{6,2},{7,3},{8,12},{9,13},{10,... | collective-permute-start | bytes 1228808 | tf_op jit(solution)/shard_map/ppermute | solution.py:24
  32.0 9.0 %collective-permute-start.6 = (bf16[80,1280]{1,0:T(8,128)(2,1)S(1)}, bf16[80,1280]{1,0:T(8,128)(2,1)S(1)}, u32[]{:S(2)}, u32[]{:S(2)}) collective-permute-start(bf16[80,1280]{1,0:T(8,128)(2,1)S(1)} %slice.287), channel_id=1, source_target_pairs={{0,4},{1,5},{2,6},{3,7},{4,0},{5,1},{6,2},{7,3},{8,12},{9,13},{10,... | collective-permute-start | bytes 614408 | tf_op jit(solution)/shard_map/ppermute | solution.py:24
  35.2 5.8 %collective-permute-start.5 = (bf16[80,1280]{1,0:T(8,128)(2,1)S(1)}, bf16[80,1280]{1,0:T(8,128)(2,1)S(1)}, u32[]{:S(2)}, u32[]{:S(2)}) collective-permute-start(bf16[80,1280]{1,0:T(8,128)(2,1)S(1)} %slice.286), channel_id=1, source_target_pairs={{0,2},{1,3},{2,0},{3,1},{4,6},{5,7},{6,4},{7,5},{8,10},{9,11},{10,... | collective-permute-start | bytes 614408 | tf_op jit(solution)/shard_map/ppermute | solution.py:24
  41.1 5.9 %collective-permute-start.7 = (bf16[640,1280]{1,0:T(8,128)(2,1)S(1)}, bf16[640,1280]{1,0:T(8,128)(2,1)}, u32[]{:S(2)}, u32[]{:S(2)}) collective-permute-start(bf16[640,1280]{1,0:T(8,128)(2,1)S(1)} %constant_dynamic-update-slice_fusion.4), channel_id=1, source_target_pairs={{0,1},{1,0},{2,3},{3,2},{4,5},{5,4},{6,7},{7,6},{8,9},{9,8},{10,11... | collective-permute-start | bytes 4915208 | tf_op jit(solution)/shard_map/ppermute | solution.py:24
  41.4 99.5 %copy-start.19 = (s32[1,256]{1,0:T(1,128)}, s32[1,256]{1,0:T(1,128)S(1)}, u32[]{:S(2)}) copy-start(s32[1,256]{1,0:T(1,128)S(1)} %pad_add_fusion.3) | copy-start | bytes 3076
  41.5 99.5 %copy-start.21 = (s32[1,256]{1,0:T(1,128)}, s32[1,256]{1,0:T(1,128)S(1)}, u32[]{:S(2)}) copy-start(s32[1,256]{1,0:T(1,128)S(1)} %pad_add_fusion.2) | copy-start | bytes 3076
  43.6 8.1 %all-to-all-start.2 = ((f32[8,8,128]{2,1,0:T(8,128)}), f32[8,8,128]{2,1,0:T(8,128)S(1)}, u32[]{:S(2)}, u32[]{:S(2)}) async-start(f32[8,8,128]{2,1,0:T(8,128)} %bitcast.156), calls=%async_computation.2 | async-start | bytes 65536 | tf_op jit(solution)/shard_map/all_to_all | solution.py:28
  51.8 17.2 %all-to-all-start.1 = ((bf16[8,40,1280]{2,1,0:T(8,128)(2,1)}), bf16[8,40,1280]{2,1,0:T(8,128)(2,1)}, u32[]{:S(2)}, u32[]{:S(2)}) async-start(bf16[8,40,1280]{2,1,0:T(8,128)(2,1)} %bitcast.11), calls=%async_computation.1 | async-start | bytes 1638400 | tf_op jit(solution)/shard_map/all_to_all | solution.py:28
  68.9 20.3 %all-to-all-start = ((bf16[8,40,1280]{2,1,0:T(8,128)(2,1)}), bf16[8,40,1280]{2,1,0:T(8,128)(2,1)}, u32[]{:S(2)}, u32[]{:S(2)}) async-start(bf16[8,40,1280]{2,1,0:T(8,128)(2,1)} %bitcast.8), calls=%async_computation | async-start | bytes 1638400 | tf_op jit(solution)/shard_map/all_to_all | solution.py:28
  74.1 31.3 %collective-permute-start.9 = (bf16[320,1280]{1,0:T(8,128)(2,1)}, bf16[320,1280]{1,0:T(8,128)(2,1)}, u32[]{:S(2)}, u32[]{:S(2)}) collective-permute-start(bf16[320,1280]{1,0:T(8,128)(2,1)} %bitcast.12), channel_id=1, source_target_pairs={{0,8},{8,0},{16,24},{24,16},{1,9},{9,1},{17,25},{25,17},{2,10},{10... | collective-permute-start | bytes 2457608 | tf_op jit(solution)/shard_map/ppermute | solution.py:24
  89.3 53.5 %all-to-all-start.5 = ((bf16[8,80,1280]{2,1,0:T(8,128)(2,1)}), bf16[8,80,1280]{2,1,0:T(8,128)(2,1)}, u32[]{:S(2)}, u32[]{:S(2)}) async-start(bf16[8,80,1280]{2,1,0:T(8,128)(2,1)} %bitcast.167), calls=%async_computation.5 | async-start | bytes 3276800 | tf_op jit(solution)/shard_map/all_to_all | solution.py:28
  95.1 52.8 %collective-permute-start.8 = (bf16[320,1280]{1,0:T(8,128)(2,1)}, bf16[320,1280]{1,0:T(8,128)(2,1)}, u32[]{:S(2)}, u32[]{:S(2)}) collective-permute-start(bf16[320,1280]{1,0:T(8,128)(2,1)} %bitcast.9), channel_id=1, source_target_pairs={{0,8},{8,0},{16,24},{24,16},{1,9},{9,1},{17,25},{25,17},{2,10},{10... | collective-permute-start | bytes 2457608 | tf_op jit(solution)/shard_map/ppermute | solution.py:24
  109.6 21.5 %collective-permute-start.15 = (bf16[128,1280]{1,0:T(8,128)(2,1)S(1)}, bf16[128,1280]{1,0:T(8,128)(2,1)S(1)}, u32[]{:S(2)}, u32[]{:S(2)}) collective-permute-start(bf16[128,1280]{1,0:T(8,128)(2,1)S(1)} %fusion.40), channel_id=1, source_target_pairs={{0,24},{8,16},{16,8},{24,0},{1,25},{9,17},{17,9},{25,1},{2,26},{10... | collective-permute-start | bytes 983048 | tf_op jit(solution)/shard_map/ppermute | solution.py:24
  110.0 31.0 %collective-permute-start.14 = (bf16[128,1280]{1,0:T(8,128)(2,1)S(1)}, bf16[128,1280]{1,0:T(8,128)(2,1)S(1)}, u32[]{:S(2)}, u32[]{:S(2)}) collective-permute-start(bf16[128,1280]{1,0:T(8,128)(2,1)S(1)} %fusion.40), channel_id=1, source_target_pairs={{0,16},{8,24},{16,0},{24,8},{1,17},{9,25},{17,1},{25,9},{2,18},{10... | collective-permute-start | bytes 983048 | tf_op jit(solution)/shard_map/ppermute | solution.py:24
  142.8 35.5 %all-to-all-start.4 = ((bf16[8,80,1280]{2,1,0:T(8,128)(2,1)}), bf16[8,80,1280]{2,1,0:T(8,128)(2,1)}, u32[]{:S(2)}, u32[]{:S(2)}) async-start(bf16[8,80,1280]{2,1,0:T(8,128)(2,1)} %bitcast.168), calls=%async_computation.4 | async-start | bytes 3276800 | tf_op jit(solution)/shard_map/all_to_all | solution.py:28
  200.0 12.8 %all-to-all-start.7 = ((f32[8,8,128]{2,1,0:T(8,128)}), f32[8,8,128]{2,1,0:T(8,128)S(1)}, u32[]{:S(2)}, u32[]{:S(2)}) async-start(f32[8,8,128]{2,1,0:T(8,128)} %copy.39), calls=%async_computation.7 | async-start | bytes 65536 | tf_op jit(solution)/shard_map/all_to_all | solution.py:28
  210.7 38.7 %collective-permute-start.13 = (bf16[320,1280]{1,0:T(8,128)(2,1)}, bf16[320,1280]{1,0:T(8,128)(2,1)S(1)}, u32[]{:S(2)}, u32[]{:S(2)}) collective-permute-start(bf16[320,1280]{1,0:T(8,128)(2,1)} %slice.291), channel_id=1, source_target_pairs={{0,8},{8,0},{16,24},{24,16},{1,9},{9,1},{17,25},{25,17},{2,10},{10... | collective-permute-start | bytes 2457608 | tf_op jit(solution)/shard_map/ppermute | solution.py:24
  210.8 77.2 %collective-permute-start.23 = (bf16[320,1280]{1,0:T(8,128)(2,1)}, bf16[320,1280]{1,0:T(8,128)(2,1)}, u32[]{:S(2)}, u32[]{:S(2)}) collective-permute-start(bf16[320,1280]{1,0:T(8,128)(2,1)} %slice.302), channel_id=1, source_target_pairs={{0,8},{8,0},{16,24},{24,16},{1,9},{9,1},{17,25},{25,17},{2,10},{10... | collective-permute-start | bytes 2457608 | tf_op jit(solution)/shard_map/ppermute | solution.py:24
  212.8 38.9 %all-to-all-start.6 = ((bf16[8,80,1280]{2,1,0:T(8,128)(2,1)}), bf16[8,80,1280]{2,1,0:T(8,128)(2,1)}, u32[]{:S(2)}, u32[]{:S(2)}) async-start(bf16[8,80,1280]{2,1,0:T(8,128)(2,1)} %bitcast.166), calls=%async_computation.6 | async-start | bytes 3276800 | tf_op jit(solution)/shard_map/all_to_all | solution.py:28
  221.8 25.3 %collective-permute-start.21 = (f32[2,128]{1,0:T(2,128)}, f32[2,128]{1,0:T(2,128)S(1)}, u32[]{:S(2)}, u32[]{:S(2)}) collective-permute-start(f32[2,128]{1,0:T(2,128)} %get-tuple-element.114), channel_id=1, source_target_pairs={{0,16},{8,24},{16,0},{24,8},{1,17},{9,25},{17,1},{25,9},{2,18},{10... | collective-permute-start | bytes 3080 | tf_op jit(solution)/shard_map/ppermute | solution.py:24
  221.8 26.8 %collective-permute-start.22 = (f32[2,128]{1,0:T(2,128)S(1)}, f32[2,128]{1,0:T(2,128)S(1)}, u32[]{:S(2)}, u32[]{:S(2)}) collective-permute-start(f32[2,128]{1,0:T(2,128)S(1)} %get-tuple-element.115), channel_id=1, source_target_pairs={{0,24},{8,16},{16,8},{24,0},{1,25},{9,17},{17,9},{25,1},{2,26},{10... | collective-permute-start | bytes 3080 | tf_op jit(solution)/shard_map/ppermute | solution.py:24
  224.2 25.1 %collective-permute-start.20 = (f32[2,128]{1,0:T(2,128)S(1)}, f32[2,128]{1,0:T(2,128)S(1)}, u32[]{:S(2)}, u32[]{:S(2)}) collective-permute-start(f32[2,128]{1,0:T(2,128)S(1)} %pad_maximum_fusion.3), channel_id=1, source_target_pairs={{0,8},{8,0},{16,24},{24,16},{1,9},{9,1},{17,25},{25,17},{2,10},{10... | collective-permute-start | bytes 3080 | tf_op jit(solution)/shard_map/ppermute | solution.py:24
  251.7 16.7 %all-to-all-start.3 = ((bf16[8,40,1280]{2,1,0:T(8,128)(2,1)}), bf16[8,40,1280]{2,1,0:T(8,128)(2,1)S(1)}, u32[]{:S(2)}, u32[]{:S(2)}) async-start(bf16[8,40,1280]{2,1,0:T(8,128)(2,1)} %bitcast.160), calls=%async_computation.3 | async-start | bytes 1638400 | tf_op jit(solution)/shard_map/all_to_all | solution.py:28
  258.6 25.1 %collective-permute-start.18 = (bf16[128,1280]{1,0:T(8,128)(2,1)}, bf16[128,1280]{1,0:T(8,128)(2,1)}, u32[]{:S(2)}, u32[]{:S(2)}) collective-permute-start(bf16[128,1280]{1,0:T(8,128)(2,1)} %get-tuple-element.90), channel_id=1, source_target_pairs={{0,16},{8,24},{16,0},{24,8},{1,17},{9,25},{17,1},{25,9},{2,18},{10... | collective-permute-start | bytes 983048 | tf_op jit(solution)/shard_map/ppermute | solution.py:24
  259.7 24.0 %collective-permute-start.19 = (bf16[128,1280]{1,0:T(8,128)(2,1)}, bf16[128,1280]{1,0:T(8,128)(2,1)}, u32[]{:S(2)}, u32[]{:S(2)}) collective-permute-start(bf16[128,1280]{1,0:T(8,128)(2,1)} %get-tuple-element.91), channel_id=1, source_target_pairs={{0,24},{8,16},{16,8},{24,0},{1,25},{9,17},{17,9},{25,1},{2,26},{10... | collective-permute-start | bytes 983048 | tf_op jit(solution)/shard_map/ppermute | solution.py:24
  268.4 26.0 %all-to-all-start.9 = ((bf16[8,80,1280]{2,1,0:T(8,128)(2,1)}), bf16[8,80,1280]{2,1,0:T(8,128)(2,1)}, u32[]{:S(2)}, u32[]{:S(2)}) async-start(bf16[8,80,1280]{2,1,0:T(8,128)(2,1)} %bitcast.165), calls=%async_computation.9 | async-start | bytes 3276800 | tf_op jit(solution)/shard_map/all_to_all | solution.py:28
  286.0 67.5 %copy-start.2 = (bf16[128,1280]{1,0:T(8,128)(2,1)}, bf16[128,1280]{1,0:T(8,128)(2,1)S(1)}, u32[]{:S(2)}) copy-start(bf16[128,1280]{1,0:T(8,128)(2,1)S(1)} %add_convert_fusion.3) | copy-start | bytes 983044
  287.9 43.3 %collective-permute-start.26 = (bf16[640,1408]{1,0:T(8,128)(2,1)}, bf16[640,1408]{1,0:T(8,128)(2,1)}, u32[]{:S(2)}, u32[]{:S(2)}) collective-permute-start(bf16[640,1408]{1,0:T(8,128)(2,1)} %pad_maximum_fusion), channel_id=1, source_target_pairs={{0,1},{1,0},{2,3},{3,2},{4,5},{5,4},{6,7},{7,6},{8,9},{9,8},{10,11... | collective-permute-start | bytes 5406728 | tf_op jit(solution)/shard_map/ppermute | solution.py:24
  294.5 24.6 %all-to-all-start.8 = ((bf16[8,40,1280]{2,1,0:T(8,128)(2,1)}), bf16[8,40,1280]{2,1,0:T(8,128)(2,1)S(1)}, u32[]{:S(2)}, u32[]{:S(2)}) async-start(bf16[8,40,1280]{2,1,0:T(8,128)(2,1)} %bitcast.159), calls=%async_computation.8 | async-start | bytes 1638400 | tf_op jit(solution)/shard_map/all_to_all | solution.py:28
  301.1 28.0 %collective-permute-start.24 = (bf16[128,1280]{1,0:T(8,128)(2,1)}, bf16[128,1280]{1,0:T(8,128)(2,1)}, u32[]{:S(2)}, u32[]{:S(2)}) collective-permute-start(bf16[128,1280]{1,0:T(8,128)(2,1)} %get-tuple-element.88), channel_id=1, source_target_pairs={{0,16},{8,24},{16,0},{24,8},{1,17},{9,25},{17,1},{25,9},{2,18},{10... | collective-permute-start | bytes 983048 | tf_op jit(solution)/shard_map/ppermute | solution.py:24
  306.2 22.9 %collective-permute-start.25 = (bf16[128,1280]{1,0:T(8,128)(2,1)}, bf16[128,1280]{1,0:T(8,128)(2,1)}, u32[]{:S(2)}, u32[]{:S(2)}) collective-permute-start(bf16[128,1280]{1,0:T(8,128)(2,1)} %get-tuple-element.89), channel_id=1, source_target_pairs={{0,24},{8,16},{16,8},{24,0},{1,25},{9,17},{17,9},{25,1},{2,26},{10... | collective-permute-start | bytes 983048 | tf_op jit(solution)/shard_map/ppermute | solution.py:24
  334.0 11.2 %collective-permute-start.27 = (bf16[320,640]{1,0:T(8,128)(2,1)S(1)}, bf16[320,640]{1,0:T(8,128)(2,1)S(1)}, u32[]{:S(2)}, u32[]{:S(2)}) collective-permute-start(bf16[320,640]{1,0:T(8,128)(2,1)S(1)} %concatenate.148), channel_id=1, source_target_pairs={{0,2},{1,3},{2,0},{3,1},{4,6},{5,7},{6,4},{7,5},{8,10},{9,11},{10,... | collective-permute-start | bytes 1228808 | tf_op jit(solution)/shard_map/ppermute | solution.py:24
  336.2 13.1 %collective-permute-start.29 = (bf16[320,768]{1,0:T(8,128)(2,1)S(1)}, bf16[320,768]{1,0:T(8,128)(2,1)S(1)}, u32[]{:S(2)}, u32[]{:S(2)}) collective-permute-start(bf16[320,768]{1,0:T(8,128)(2,1)S(1)} %maximum_maximum_fusion), channel_id=1, source_target_pairs={{0,4},{1,5},{2,6},{3,7},{4,0},{5,1},{6,2},{7,3},{8,12},{9,13},{10,... | collective-permute-start | bytes 1474568 | tf_op jit(solution)/shard_map/ppermute | solution.py:24
  345.3 7.1 %collective-permute-start.28 = (bf16[160,640]{1,0:T(8,128)(2,1)S(1)}, bf16[160,640]{1,0:T(8,128)(2,1)S(1)}, u32[]{:S(2)}, u32[]{:S(2)}) collective-permute-start(bf16[160,640]{1,0:T(8,128)(2,1)S(1)} %fusion.43), channel_id=1, source_target_pairs={{0,4},{1,5},{2,6},{3,7},{4,0},{5,1},{6,2},{7,3},{8,12},{9,13},{10,... | collective-permute-start | bytes 614408 | tf_op jit(solution)/shard_map/ppermute | solution.py:24
  352.7 6.8 %collective-permute-start.30 = (bf16[160,768]{1,0:T(8,128)(2,1)S(1)}, bf16[160,768]{1,0:T(8,128)(2,1)S(1)}, u32[]{:S(2)}, u32[]{:S(2)}) collective-permute-start(bf16[160,768]{1,0:T(8,128)(2,1)S(1)} %fusion.41), channel_id=1, source_target_pairs={{0,2},{1,3},{2,0},{3,1},{4,6},{5,7},{6,4},{7,5},{8,10},{9,11},{10,... | collective-permute-start | bytes 737288 | tf_op jit(solution)/shard_map/ppermute | solution.py:24
  359.7 12.1 %collective-permute-start.31 = (bf16[40,1408]{1,0:T(8,128)(2,1)S(1)}, bf16[40,1408]{1,0:T(8,128)(2,1)S(1)}, u32[]{:S(2)}, u32[]{:S(2)}) collective-permute-start(bf16[40,1408]{1,0:T(8,128)(2,1)S(1)} %get-tuple-element.92), channel_id=1, source_target_pairs={{0,8},{8,0},{16,24},{24,16},{1,9},{9,1},{17,25},{25,17},{2,10},{10... | collective-permute-start | bytes 337928 | tf_op jit(solution)/shard_map/ppermute | solution.py:24
  367.5 7.2 %collective-permute-start.33 = (bf16[40,1408]{1,0:T(8,128)(2,1)S(1)}, bf16[40,1408]{1,0:T(8,128)(2,1)S(1)}, u32[]{:S(2)}, u32[]{:S(2)}) collective-permute-start(bf16[40,1408]{1,0:T(8,128)(2,1)S(1)} %get-tuple-element.93), channel_id=1, source_target_pairs={{0,24},{8,16},{16,8},{24,0},{1,25},{9,17},{17,9},{25,1},{2,26},{10... | collective-permute-start | bytes 337928 | tf_op jit(solution)/shard_map/ppermute | solution.py:24
  369.0 9.3 %collective-permute-start.32 = (bf16[40,1408]{1,0:T(8,128)(2,1)S(1)}, bf16[40,1408]{1,0:T(8,128)(2,1)S(1)}, u32[]{:S(2)}, u32[]{:S(2)}) collective-permute-start(bf16[40,1408]{1,0:T(8,128)(2,1)S(1)} %get-tuple-element.94), channel_id=1, source_target_pairs={{0,16},{8,24},{16,0},{24,8},{1,17},{9,25},{17,1},{25,9},{2,18},{10... | collective-permute-start | bytes 337928 | tf_op jit(solution)/shard_map/ppermute | solution.py:24
  (21 other events, 119.2 us)
where the time goes:
time: 381 us; the launch traced here: 380 us
  waiting for transfers between devices  121 us (32%)
  starting transfers between devices  115 us (30%)
  Pallas kernels  63.2 us (17%)
  matrix products  50.9 us (13%)
  other arithmetic  14.4 us (4%)
  local copies, waits for them, and re-layouts  13.8 us (4%)
    ppermute x34, waiting for transfers between devices, swap(): return lax.ppermute(value, axis, [(i, i ^ bit) for i in range(n)])  99.2 us
    ppermute x34, starting transfers between devices, swap(): return lax.ppermute(value, axis, [(i, i ^ bit) for i in range(n)])  74.3 us
    dot_general x38, matrix products, dot32(): lax.dot_general(a, b, (dims, ((), ())), preferred_element_type=F32, preci...  50.9 us
    all_to_all x10, starting transfers between devices, exchange(): lax.all_to_all(value, 'expert', split_axis=0, concat_axis=0, tiled=True)  40.5 us
    pallas_call x2, Pallas kernels, ffn(): pl.pallas_call(functools.partial(ffn_kernel, chunk_of(hidden, 256)), grid...  40.4 us
    pallas_call x2, Pallas kernels, wgrad(): pl.pallas_call(functools.partial(wgrad_kernel, scale, len(lefts)), grid=(...  22.8 us
    all_to_all x10, waiting for transfers between devices, exchange(): lax.all_to_all(value, 'expert', split_axis=0, concat_axis=0, tiled=True)  22.1 us
  transfers between devices with their start and end apart: 44, of which 23 were waited for; matrix products, arithmetic and copies ran while one was open for 18% of the time, Pallas kernels for 11%

commit v1 on v0

--- a/solution.py
+++ b/solution.py
@@ -354,9 +354,10 @@
 
     half = width // 2
     sent = jnp.concatenate([v.astype(BF) for v in sums_of(slice(half, width))], axis=1)
-    got = swap(sent, "expert", 1).astype(F32)
+    got = swap(sent, "expert", 1)
     part_out, part_router = sums_of(slice(0, half))
-    part_out, part_router = part_out + got[:, :width], part_router + got[:, width:]
+    part_out = part_out + got[:, :width].astype(F32)
+    part_router = part_router + got[:, width:].astype(F32)
     bit = 2
     while bit < lo:
         half = half // 2
@@ -370,11 +371,12 @@
         jnp.concatenate([part_out[i * rows_q : (i + 1) * rows_q, mid:], part_router[i * rows_q : (i + 1) * rows_q]], axis=1)
         for i in range(4)
     ]
-    got_l = swap(jnp.concatenate([left[2], left[3]], axis=0).astype(BF), "expert", lo).astype(F32)
-    got_r = swap(jnp.concatenate([right[1], right[3]], axis=0).astype(BF), "expert", hi).astype(F32)
-    fin_l = swap((left[1] + got_l[rows_q:]).astype(BF), "expert", hi).astype(F32)
-    fin_r = swap((right[2] + got_r[rows_q:]).astype(BF), "expert", lo).astype(F32)
-    kept = jnp.concatenate([left[0] + got_l[:rows_q] + fin_l, right[0] + got_r[:rows_q] + fin_r], axis=1)
+    got_l = swap(jnp.concatenate([left[2], left[3]], axis=0).astype(BF), "expert", lo)
+    got_r = swap(jnp.concatenate([right[1], right[3]], axis=0).astype(BF), "expert", hi)
+    fin_l = swap((left[1] + got_l[rows_q:].astype(F32)).astype(BF), "expert", hi).astype(F32)
+    fin_r = swap((right[2] + got_r[rows_q:].astype(F32)).astype(BF), "expert", lo).astype(F32)
+    fin_l, fin_r = lax.optimization_barrier((fin_l, fin_r))
+    kept = jnp.concatenate([left[0] + got_l[:rows_q].astype(F32) + fin_l, right[0] + got_r[:rows_q].astype(F32) + fin_r], axis=1)
     grads = kept[:shard]
     for j in range(1, n_dp):
         grads = grads + swap(kept[j * shard : (j + 1) * shard].astype(BF), "dp", j).astype(F32)

time: 381 us -> 377 us (0.990)
  waiting for transfers between devices: 121 us -> 116 us
    ppermute x34, waiting for transfers between devices: 99.2 us -> 93.5 us  [swap(): return lax.ppermute(value, axis, [(i, i ^ bit) for i in range(n)])]
  transfers between devices with their start and end apart: 44 -> 44, of which waited for: 23 -> 21; matrix products, arithmetic and copies ran while one was open for 18% -> 18% of each run, Pallas kernels for 11% -> 12%
where the time goes in v1:
time: 377 us; the launch traced here: 375 us
  waiting for transfers between devices  116 us (31%)
  starting transfers between devices  115 us (31%)
  Pallas kernels  63.1 us (17%)
  matrix products  53.2 us (14%)
  local copies, waits for them, and re-layouts  14.7 us (4%)
  other arithmetic  12.4 us (3%)
    ppermute x34, waiting for transfers between devices, swap(): return lax.ppermute(value, axis, [(i, i ^ bit) for i in range(n)])  93.5 us
    ppermute x34, starting transfers between devices, swap(): return lax.ppermute(value, axis, [(i, i ^ bit) for i in range(n)])  74.2 us
    dot_general x38, matrix products, dot32(): lax.dot_general(a, b, (dims, ((), ())), preferred_element_type=F32, preci...  53.2 us
    all_to_all x10, starting transfers between devices, exchange(): lax.all_to_all(value, 'expert', split_axis=0, concat_axis=0, tiled=True)  40.5 us
    pallas_call x2, Pallas kernels, ffn(): pl.pallas_call(functools.partial(ffn_kernel, chunk_of(hidden, 256)), grid...  40.4 us
    pallas_call x2, Pallas kernels, wgrad(): pl.pallas_call(functools.partial(wgrad_kernel, scale, len(lefts)), grid=(...  22.8 us
    all_to_all x10, waiting for transfers between devices, exchange(): lax.all_to_all(value, 'expert', split_axis=0, concat_axis=0, tiled=True)  22.1 us
  transfers between devices with their start and end apart: 44, of which 21 were waited for; matrix products, arithmetic and copies ran while one was open for 18% of the time, Pallas kernels for 12%

profile of v1, /device:TPU:0, one launch (start us, length us, event | category | flops | bytes accessed | tf_op | source)
XLA Modules:
  0.0 375.3 jit_solution(8547981841165728609)
XLA Ops:
  0.6 5.1 %collective-permute-start.12 = (s32[2,128]{1,0:T(2,128)}, s32[2,128]{1,0:T(2,128)S(1)}, u32[]{:S(2)}, u32[]{:S(2)}) collective-permute-start(s32[2,128]{1,0:T(2,128)} %bitcast.177), channel_id=1, source_target_pairs={{0,24},{8,16},{16,8},{24,0},{1,25},{9,17},{17,9},{25,1},{2,26},{10... | collective-permute-start | bytes 3080 | tf_op jit(solution)/shard_map/ppermute | solution.py:24
  6.4 2.3 collective-permute-start.1
  15.0 3.7 collective-permute-start.17
  19.2 3.3 collective-permute-done.2
  26.5 5.5 %collective-permute-done.4 = bf16[160,1280]{1,0:T(8,128)(2,1)S(1)} collective-permute-done((bf16[160,1280]{1,0:T(8,128)(2,1)}, bf16[160,1280]{1,0:T(8,128)(2,1)S(1)}, u32[]{:S(2)}, u32[]{:S(2)}) %collective-permute-start.4) | collective-permute-done | bytes 409632 | tf_op jit(solution)/shard_map/ppermute | solution.py:24
  36.3 4.8 %collective-permute-done.5 = bf16[80,1280]{1,0:T(8,128)(2,1)S(1)} collective-permute-done((bf16[80,1280]{1,0:T(8,128)(2,1)S(1)}, bf16[80,1280]{1,0:T(8,128)(2,1)S(1)}, u32[]{:S(2)}, u32[]{:S(2)}) %collective-permute-start.5) | collective-permute-done | bytes 204832 | tf_op jit(solution)/shard_map/ppermute | solution.py:24
  43.7 3.3 all-to-all-start.2
  51.8 4.2 %all-to-all-start.1 = ((bf16[8,40,1280]{2,1,0:T(8,128)(2,1)}), bf16[8,40,1280]{2,1,0:T(8,128)(2,1)}, u32[]{:S(2)}, u32[]{:S(2)}) async-start(bf16[8,40,1280]{2,1,0:T(8,128)(2,1)} %bitcast.11), calls=%async_computation.1 | async-start | bytes 1638400 | tf_op jit(solution)/shard_map/all_to_all | solution.py:28
  57.5 11.5 %all-to-all-done.1 = bf16[8,40,1280]{2,1,0:T(8,128)(2,1)} async-done(((bf16[8,40,1280]{2,1,0:T(8,128)(2,1)}), bf16[8,40,1280]{2,1,0:T(8,128)(2,1)}, u32[]{:S(2)}, u32[]{:S(2)}) %all-to-all-start.1) | async-done | bytes 819232 | tf_op jit(solution)/shard_map/all_to_all | solution.py:28
  69.0 4.2 %all-to-all-start = ((bf16[8,40,1280]{2,1,0:T(8,128)(2,1)}), bf16[8,40,1280]{2,1,0:T(8,128)(2,1)}, u32[]{:S(2)}, u32[]{:S(2)}) async-start(bf16[8,40,1280]{2,1,0:T(8,128)(2,1)} %bitcast.8), calls=%async_computation | async-start | bytes 1638400 | tf_op jit(solution)/shard_map/all_to_all | solution.py:28
  74.2 12.2 %collective-permute-start.9 = (bf16[320,1280]{1,0:T(8,128)(2,1)}, bf16[320,1280]{1,0:T(8,128)(2,1)}, u32[]{:S(2)}, u32[]{:S(2)}) collective-permute-start(bf16[320,1280]{1,0:T(8,128)(2,1)} %bitcast.12), channel_id=1, source_target_pairs={{0,8},{8,0},{16,24},{24,16},{1,9},{9,1},{17,25},{25,17},{2,10},{10... | collective-permute-start | bytes 2457608 | tf_op jit(solution)/shard_map/ppermute | solution.py:24
  86.4 2.9 convolution_convert_fusion.1
  89.3 4.3 %all-to-all-start.5 = ((bf16[8,80,1280]{2,1,0:T(8,128)(2,1)}), bf16[8,80,1280]{2,1,0:T(8,128)(2,1)}, u32[]{:S(2)}, u32[]{:S(2)}) async-start(bf16[8,80,1280]{2,1,0:T(8,128)(2,1)} %bitcast.167), calls=%async_computation.5 | async-start | bytes 3276800 | tf_op jit(solution)/shard_map/all_to_all | solution.py:28
  95.2 9.1 %collective-permute-start.8 = (bf16[320,1280]{1,0:T(8,128)(2,1)}, bf16[320,1280]{1,0:T(8,128)(2,1)}, u32[]{:S(2)}, u32[]{:S(2)}) collective-permute-start(bf16[320,1280]{1,0:T(8,128)(2,1)} %bitcast.9), channel_id=1, source_target_pairs={{0,8},{8,0},{16,24},{24,16},{1,9},{9,1},{17,25},{25,17},{2,10},{10... | collective-permute-start | bytes 2457608 | tf_op jit(solution)/shard_map/ppermute | solution.py:24
  105.5 4.1 %convolution_convert_fusion.5 = bf16[640,1280]{1,0:T(8,128)(2,1)} fusion(bf16[320,1280]{1,0:T(8,128)(2,1)} %collective-permute-done.9, bf16[320,1280]{1,0:T(8,128)(2,1)} %bitcast.12, s32[640]{0:T(1024)S(1)} %fusion.161), kind=kOutput, calls=%fused_computation.14 | convolution fusion | flops 1053081600 | bytes 3279360 | tf_op jit(solution)/shard_map/dot_general | solution.py:17
  110.1 2.8 collective-permute-start.14
  113.0 2.2 fusion.13
  115.3 15.9 %collective-permute-done.15 = bf16[128,1280]{1,0:T(8,128)(2,1)S(1)} collective-permute-done((bf16[128,1280]{1,0:T(8,128)(2,1)S(1)}, bf16[128,1280]{1,0:T(8,128)(2,1)S(1)}, u32[]{:S(2)}, u32[]{:S(2)}) %collective-permute-start.15) | collective-permute-done | bytes 327712 | tf_op jit(solution)/shard_map/ppermute | solution.py:24
  131.1 9.9 %collective-permute-done.14 = bf16[128,1280]{1,0:T(8,128)(2,1)S(1)} collective-permute-done((bf16[128,1280]{1,0:T(8,128)(2,1)S(1)}, bf16[128,1280]{1,0:T(8,128)(2,1)S(1)}, u32[]{:S(2)}, u32[]{:S(2)}) %collective-permute-start.14) | collective-permute-done | bytes 327712 | tf_op jit(solution)/shard_map/ppermute | solution.py:24
  142.8 4.5 %all-to-all-start.4 = ((bf16[8,80,1280]{2,1,0:T(8,128)(2,1)}), bf16[8,80,1280]{2,1,0:T(8,128)(2,1)}, u32[]{:S(2)}, u32[]{:S(2)}) async-start(bf16[8,80,1280]{2,1,0:T(8,128)(2,1)} %bitcast.168), calls=%async_computation.4 | async-start | bytes 3276800 | tf_op jit(solution)/shard_map/all_to_all | solution.py:28
  147.9 4.1 %convolution_convert_fusion.6 = bf16[640,1280]{1,0:T(8,128)(2,1)} fusion(bf16[320,1280]{1,0:T(8,128)(2,1)} %collective-permute-done.8, bf16[320,1280]{1,0:T(8,128)(2,1)} %bitcast.9, s32[640]{0:T(1024)S(1)} %fusion.161), kind=kOutput, calls=%fused_computation.15 | convolution fusion | flops 1053081600 | bytes 3279360 | tf_op jit(solution)/shard_map/dot_general | solution.py:17
  152.0 20.8 %shard_map.135 = (bf16[2,320,1280]{2,1,0:T(8,128)(2,1)}, bf16[2,320,1280]{2,1,0:T(8,128)(2,1)}, bf16[2,320,1280]{2,1,0:T(8,128)(2,1)}, bf16[2,320,1280]{2,1,0:T(8,128)(2,1)}, f32[2,320,1]{2,1,0:T(8,128)}) custom-call(bf16[2,320,1280]{2,1,0:T(8,128)(2,1)} %bitcast.163, bf16[2,320,1280]{2,1,0:T(8,128)(2,1)} %bitcast.161, ...), custom_call_target="tpu_custom_call" | custom-call | flops 8388608000 | bytes 26214400 | tf_op jit(solution)/shard_map/pallas_call | solution.py:86
  174.1 4.1 %convolution_convert_fusion.4 = bf16[640,1280]{1,0:T(8,128)(2,1)} fusion(bf16[640,1280]{1,0:T(8,128)(2,1)} %bitcast.206, s32[640]{0:T(1024)S(1)} %fusion.161), kind=kOutput, calls=%fused_computation.13 | convolution fusion | flops 1049804800 | bytes 3279360 | tf_op jit(solution)/shard_map/dot_general | solution.py:17
  178.3 19.6 %shard_map.136 = (bf16[8,2,40,1280]{3,2,1,0:T(8,128)(2,1)}, bf16[8,2,40,1280]{3,2,1,0:T(8,128)(2,1)}, bf16[2,320,1280]{2,1,0:T(8,128)(2,1)}, bf16[2,320,1280]{2,1,0:T(8,128)(2,1)}, f32[2,320,1]{2,1,0:T(8,128)}) custom-call(bf16[8,2,40,1280]{3,2,1,0:T(8,128)(2,1)} %bitcast.39.x_ref.refs_1_, bf16[8,2,40,1280]{3,2,1,0:T(8,128)(2,1)} %bitcast.41.c_ref.refs_3_, ...), custom_call_target="tpu_custom_call" | custom-call | flops 8388608000 | bytes 26214400 | tf_op jit(solution)/shard_map/pallas_call | solution.py:86
  199.9 3.9 %all-to-all-start.7 = ((f32[8,8,128]{2,1,0:T(8,128)}), f32[8,8,128]{2,1,0:T(8,128)S(1)}, u32[]{:S(2)}, u32[]{:S(2)}) async-start(f32[8,8,128]{2,1,0:T(8,128)} %copy.39), calls=%async_computation.7 | async-start | bytes 65536 | tf_op jit(solution)/shard_map/all_to_all | solution.py:28
  203.9 3.0 convolution_convert_fusion.3
  212.8 4.3 %all-to-all-start.6 = ((bf16[8,80,1280]{2,1,0:T(8,128)(2,1)}), bf16[8,80,1280]{2,1,0:T(8,128)(2,1)}, u32[]{:S(2)}, u32[]{:S(2)}) async-start(bf16[8,80,1280]{2,1,0:T(8,128)(2,1)} %bitcast.166), calls=%async_computation.6 | async-start | bytes 3276800 | tf_op jit(solution)/shard_map/all_to_all | solution.py:28
  221.8 2.4 collective-permute-start.22
  225.3 11.4 %shard_map.137 = f32[2,1280,1280]{2,1,0:T(8,128)} custom-call(bf16[2,320,1280]{2,1,0:T(8,128)(2,1)} %bitcast.164, bf16[8,2,40,1280]{3,2,1,0:T(8,128)(2,1)} %bitcast.39.x_ref.refs_1_, bf16[2,320,1280]{2,1,0:T(8,128)(2,1)} %get-tuple-element.39.refs_2_, bf16[2,320,1280]{2,1,0:T(8,128)(2,1)} %get-tuple-element.40.refs_3_), custom_call_target="tpu_custom_call" | custom-call | flops 4194304000 | bytes 19660800 | tf_op jit(solution)/shard_map/pallas_call | solution.py:126
  236.7 10.4 %collective-permute-done.21 = f32[2,128]{1,0:T(2,128)S(1)} collective-permute-done((f32[2,128]{1,0:T(2,128)}, f32[2,128]{1,0:T(2,128)S(1)}, u32[]{:S(2)}, u32[]{:S(2)}) %collective-permute-start.21) | collective-permute-done | bytes 1056 | tf_op jit(solution)/shard_map/ppermute | solution.py:24
  249.4 2.2 add_convert_fusion.1
  251.7 3.8 %all-to-all-start.3 = ((bf16[8,40,1280]{2,1,0:T(8,128)(2,1)}), bf16[8,40,1280]{2,1,0:T(8,128)(2,1)S(1)}, u32[]{:S(2)}, u32[]{:S(2)}) async-start(bf16[8,40,1280]{2,1,0:T(8,128)(2,1)} %bitcast.160), calls=%async_computation.3 | async-start | bytes 1638400 | tf_op jit(solution)/shard_map/all_to_all | solution.py:28
  263.5 5.0 %all-to-all-done.3 = bf16[8,40,1280]{2,1,0:T(8,128)(2,1)S(1)} async-done(((bf16[8,40,1280]{2,1,0:T(8,128)(2,1)}), bf16[8,40,1280]{2,1,0:T(8,128)(2,1)S(1)}, u32[]{:S(2)}, u32[]{:S(2)}) %all-to-all-start.3) | async-done | bytes 819232 | tf_op jit(solution)/shard_map/all_to_all | solution.py:28
  268.4 4.3 %all-to-all-start.9 = ((bf16[8,80,1280]{2,1,0:T(8,128)(2,1)}), bf16[8,80,1280]{2,1,0:T(8,128)(2,1)}, u32[]{:S(2)}, u32[]{:S(2)}) async-start(bf16[8,80,1280]{2,1,0:T(8,128)(2,1)} %bitcast.165), calls=%async_computation.9 | async-start | bytes 3276800 | tf_op jit(solution)/shard_map/all_to_all | solution.py:28
  272.8 10.9 %collective-permute-done.18 = bf16[128,1280]{1,0:T(8,128)(2,1)} collective-permute-done((bf16[128,1280]{1,0:T(8,128)(2,1)}, bf16[128,1280]{1,0:T(8,128)(2,1)}, u32[]{:S(2)}, u32[]{:S(2)}) %collective-permute-start.18) | collective-permute-done | bytes 327712 | tf_op jit(solution)/shard_map/ppermute | solution.py:24
  288.7 2.3 add_convert_fusion
  290.9 3.6 all-to-all-done.9
  294.5 3.5 all-to-all-start.8
  301.1 5.1 %collective-permute-start.24 = (bf16[128,1280]{1,0:T(8,128)(2,1)}, bf16[128,1280]{1,0:T(8,128)(2,1)}, u32[]{:S(2)}, u32[]{:S(2)}) collective-permute-start(bf16[128,1280]{1,0:T(8,128)(2,1)} %get-tuple-element.93), channel_id=1, source_target_pairs={{0,16},{8,24},{16,0},{24,8},{1,17},{9,25},{17,1},{25,9},{2,18},{10... | collective-permute-start | bytes 983048 | tf_op jit(solution)/shard_map/ppermute | solution.py:24
  307.7 11.4 %shard_map.138 = f32[2,1280,1280]{2,1,0:T(8,128)} custom-call(bf16[2,320,1280]{2,1,0:T(8,128)(2,1)} %get-tuple-element.41.refs_0_, bf16[2,320,1280]{2,1,0:T(8,128)(2,1)} %get-tuple-element.42.refs_1_, bf16[2,320,1280]{2,1,0:T(8,128)(2,1)} %bitcast.162, bf16[8,2,40,1280]{3,2,1,0:T(8,128)(2,1)} %bitcast.41.c_ref.refs_3_), custom_call_target="tpu_custom_call" | custom-call | flops 4194304000 | bytes 19660800 | tf_op jit(solution)/shard_map/pallas_call | solution.py:126
  319.0 10.0 %collective-permute-done.24 = bf16[128,1280]{1,0:T(8,128)(2,1)} collective-permute-done((bf16[128,1280]{1,0:T(8,128)(2,1)}, bf16[128,1280]{1,0:T(8,128)(2,1)}, u32[]{:S(2)}, u32[]{:S(2)}) %collective-permute-start.24) | collective-permute-done | bytes 327712 | tf_op jit(solution)/shard_map/ppermute | solution.py:24
  329.0 2.2 add_convert_fusion.2
  339.7 6.8 %collective-permute-done.27 = bf16[320,640]{1,0:T(8,128)(2,1)S(1)} collective-permute-done((bf16[320,640]{1,0:T(8,128)(2,1)S(1)}, bf16[320,640]{1,0:T(8,128)(2,1)S(1)}, u32[]{:S(2)}, u32[]{:S(2)}) %collective-permute-start.27) | collective-permute-done | bytes 409632 | tf_op jit(solution)/shard_map/ppermute | solution.py:24
  348.0 2.7 collective-permute-done.29
  354.0 3.0 collective-permute-done.30
  357.3 7.5 %collective-permute-start.31 = (bf16[40,1408]{1,0:T(8,128)(2,1)S(1)}, bf16[40,1408]{1,0:T(8,128)(2,1)S(1)}, u32[]{:S(2)}, u32[]{:S(2)}) collective-permute-start(bf16[40,1408]{1,0:T(8,128)(2,1)S(1)} %get-tuple-element.97), channel_id=1, source_target_pairs={{0,8},{8,0},{16,24},{24,16},{1,9},{9,1},{17,25},{25,17},{2,10},{10... | collective-permute-start | bytes 337928 | tf_op jit(solution)/shard_map/ppermute | solution.py:24
  368.5 2.9 collective-permute-done.33
  371.4 2.4 collective-permute-done.32
  (236 shorter events, 84.3 us)
Async XLA Ops:
  0.6 14.2 %collective-permute-start.12 = (s32[2,128]{1,0:T(2,128)}, s32[2,128]{1,0:T(2,128)S(1)}, u32[]{:S(2)}, u32[]{:S(2)}) collective-permute-start(s32[2,128]{1,0:T(2,128)} %bitcast.177), channel_id=1, source_target_pairs={{0,24},{8,16},{16,8},{24,0},{1,25},{9,17},{17,9},{25,1},{2,26},{10... | collective-permute-start | bytes 3080 | tf_op jit(solution)/shard_map/ppermute | solution.py:24
  5.8 9.3 %collective-permute-start.11 = (s32[2,128]{1,0:T(2,128)}, s32[2,128]{1,0:T(2,128)S(1)}, u32[]{:S(2)}, u32[]{:S(2)}) collective-permute-start(s32[2,128]{1,0:T(2,128)} %bitcast.178), channel_id=1, source_target_pairs={{0,16},{8,24},{16,0},{24,8},{1,17},{9,25},{17,1},{25,9},{2,18},{10... | collective-permute-start | bytes 3080 | tf_op jit(solution)/shard_map/ppermute | solution.py:24
  5.8 13.0 %collective-permute-start.10 = (s32[2,128]{1,0:T(2,128)}, s32[2,128]{1,0:T(2,128)S(1)}, u32[]{:S(2)}, u32[]{:S(2)}) collective-permute-start(s32[2,128]{1,0:T(2,128)} %bitcast.179), channel_id=1, source_target_pairs={{0,8},{8,0},{16,24},{24,16},{1,9},{9,1},{17,25},{25,17},{2,10},{10... | collective-permute-start | bytes 3080 | tf_op jit(solution)/shard_map/ppermute | solution.py:24
  6.4 12.8 %collective-permute-start.1 = (bf16[40,1280]{1,0:T(8,128)(2,1)}, bf16[40,1280]{1,0:T(8,128)(2,1)S(1)}, u32[]{:S(2)}, u32[]{:S(2)}) collective-permute-start(bf16[40,1280]{1,0:T(8,128)(2,1)} %param.10), channel_id=1, source_target_pairs={{0,16},{8,24},{16,0},{24,8},{1,17},{9,25},{17,1},{25,9},{2,18},{10... | collective-permute-start | bytes 307208 | tf_op jit(solution)/shard_map/ppermute | solution.py:24
  8.7 10.5 %collective-permute-start = (bf16[40,1280]{1,0:T(8,128)(2,1)}, bf16[40,1280]{1,0:T(8,128)(2,1)S(1)}, u32[]{:S(2)}, u32[]{:S(2)}) collective-permute-start(bf16[40,1280]{1,0:T(8,128)(2,1)} %param.10), channel_id=1, source_target_pairs={{0,8},{8,0},{16,24},{24,16},{1,9},{9,1},{17,25},{25,17},{2,10},{10... | collective-permute-start | bytes 307208 | tf_op jit(solution)/shard_map/ppermute | solution.py:24
  13.6 272.4 %copy-start.6 = (bf16[128,1280]{0,1:T(8,128)(2,1)}, bf16[128,1280]{0,1:T(8,128)(2,1)S(1)}, u32[]{:S(2)}) copy-start(bf16[128,1280]{0,1:T(8,128)(2,1)S(1)} %fusion.14) | copy-start | bytes 983044
  14.9 7.7 %collective-permute-start.2 = (bf16[40,1280]{1,0:T(8,128)(2,1)S(1)}, bf16[40,1280]{1,0:T(8,128)(2,1)S(1)}, u32[]{:S(2)}, u32[]{:S(2)}) collective-permute-start(bf16[40,1280]{1,0:T(8,128)(2,1)S(1)} %copy-done.13), channel_id=1, source_target_pairs={{0,24},{8,16},{16,8},{24,0},{1,25},{9,17},{17,9},{25,1},{2,26},{10... | collective-permute-start | bytes 307208 | tf_op jit(solution)/shard_map/ppermute | solution.py:24
  15.0 71.4 %collective-permute-start.17 = (bf16[128,1280]{1,0:T(8,128)(2,1)S(1)}, bf16[128,1280]{1,0:T(8,128)(2,1)}, u32[]{:S(2)}, u32[]{:S(2)}) collective-permute-start(bf16[128,1280]{1,0:T(8,128)(2,1)S(1)} %copy-done.8), channel_id=1, source_target_pairs={{0,24},{8,16},{16,8},{24,0},{1,25},{9,17},{17,9},{25,1},{2,26},{10... | collective-permute-start | bytes 983048 | tf_op jit(solution)/shard_map/ppermute | solution.py:24
  18.8 67.7 %collective-permute-start.16 = (bf16[128,1280]{1,0:T(8,128)(2,1)S(1)}, bf16[128,1280]{1,0:T(8,128)(2,1)}, u32[]{:S(2)}, u32[]{:S(2)}) collective-permute-start(bf16[128,1280]{1,0:T(8,128)(2,1)S(1)} %copy-done.8), channel_id=1, source_target_pairs={{0,16},{8,24},{16,0},{24,8},{1,17},{9,25},{17,1},{25,9},{2,18},{10... | collective-permute-start | bytes 983048 | tf_op jit(solution)/shard_map/ppermute | solution.py:24
  23.3 8.7 %collective-permute-start.4 = (bf16[160,1280]{1,0:T(8,128)(2,1)}, bf16[160,1280]{1,0:T(8,128)(2,1)S(1)}, u32[]{:S(2)}, u32[]{:S(2)}) collective-permute-start(bf16[160,1280]{1,0:T(8,128)(2,1)} %copy-done.16), channel_id=1, source_target_pairs={{0,2},{1,3},{2,0},{3,1},{4,6},{5,7},{6,4},{7,5},{8,10},{9,11},{10,... | collective-permute-start | bytes 1228808 | tf_op jit(solution)/shard_map/ppermute | solution.py:24
  24.8 10.4 %collective-permute-start.3 = (bf16[160,1280]{1,0:T(8,128)(2,1)}, bf16[160,1280]{1,0:T(8,128)(2,1)S(1)}, u32[]{:S(2)}, u32[]{:S(2)}) collective-permute-start(bf16[160,1280]{1,0:T(8,128)(2,1)} %copy-done.16), channel_id=1, source_target_pairs={{0,4},{1,5},{2,6},{3,7},{4,0},{5,1},{6,2},{7,3},{8,12},{9,13},{10,... | collective-permute-start | bytes 1228808 | tf_op jit(solution)/shard_map/ppermute | solution.py:24
  32.0 9.0 %collective-permute-start.6 = (bf16[80,1280]{1,0:T(8,128)(2,1)S(1)}, bf16[80,1280]{1,0:T(8,128)(2,1)S(1)}, u32[]{:S(2)}, u32[]{:S(2)}) collective-permute-start(bf16[80,1280]{1,0:T(8,128)(2,1)S(1)} %slice.287), channel_id=1, source_target_pairs={{0,4},{1,5},{2,6},{3,7},{4,0},{5,1},{6,2},{7,3},{8,12},{9,13},{10,... | collective-permute-start | bytes 614408 | tf_op jit(solution)/shard_map/ppermute | solution.py:24
  35.2 5.8 %collective-permute-start.5 = (bf16[80,1280]{1,0:T(8,128)(2,1)S(1)}, bf16[80,1280]{1,0:T(8,128)(2,1)S(1)}, u32[]{:S(2)}, u32[]{:S(2)}) collective-permute-start(bf16[80,1280]{1,0:T(8,128)(2,1)S(1)} %slice.286), channel_id=1, source_target_pairs={{0,2},{1,3},{2,0},{3,1},{4,6},{5,7},{6,4},{7,5},{8,10},{9,11},{10,... | collective-permute-start | bytes 614408 | tf_op jit(solution)/shard_map/ppermute | solution.py:24
  41.1 6.0 %collective-permute-start.7 = (bf16[640,1280]{1,0:T(8,128)(2,1)S(1)}, bf16[640,1280]{1,0:T(8,128)(2,1)}, u32[]{:S(2)}, u32[]{:S(2)}) collective-permute-start(bf16[640,1280]{1,0:T(8,128)(2,1)S(1)} %constant_dynamic-update-slice_fusion.4), channel_id=1, source_target_pairs={{0,1},{1,0},{2,3},{3,2},{4,5},{5,4},{6,7},{7,6},{8,9},{9,8},{10,11... | collective-permute-start | bytes 4915208 | tf_op jit(solution)/shard_map/ppermute | solution.py:24
  41.4 99.6 %copy-start.19 = (s32[1,256]{1,0:T(1,128)}, s32[1,256]{1,0:T(1,128)S(1)}, u32[]{:S(2)}) copy-start(s32[1,256]{1,0:T(1,128)S(1)} %pad_add_fusion.3) | copy-start | bytes 3076
  41.5 99.6 %copy-start.21 = (s32[1,256]{1,0:T(1,128)}, s32[1,256]{1,0:T(1,128)S(1)}, u32[]{:S(2)}) copy-start(s32[1,256]{1,0:T(1,128)S(1)} %pad_add_fusion.2) | copy-start | bytes 3076
  43.7 8.1 %all-to-all-start.2 = ((f32[8,8,128]{2,1,0:T(8,128)}), f32[8,8,128]{2,1,0:T(8,128)S(1)}, u32[]{:S(2)}, u32[]{:S(2)}) async-start(f32[8,8,128]{2,1,0:T(8,128)} %bitcast.156), calls=%async_computation.2 | async-start | bytes 65536 | tf_op jit(solution)/shard_map/all_to_all | solution.py:28
  51.8 17.2 %all-to-all-start.1 = ((bf16[8,40,1280]{2,1,0:T(8,128)(2,1)}), bf16[8,40,1280]{2,1,0:T(8,128)(2,1)}, u32[]{:S(2)}, u32[]{:S(2)}) async-start(bf16[8,40,1280]{2,1,0:T(8,128)(2,1)} %bitcast.11), calls=%async_computation.1 | async-start | bytes 1638400 | tf_op jit(solution)/shard_map/all_to_all | solution.py:28
  69.0 20.3 %all-to-all-start = ((bf16[8,40,1280]{2,1,0:T(8,128)(2,1)}), bf16[8,40,1280]{2,1,0:T(8,128)(2,1)}, u32[]{:S(2)}, u32[]{:S(2)}) async-start(bf16[8,40,1280]{2,1,0:T(8,128)(2,1)} %bitcast.8), calls=%async_computation | async-start | bytes 1638400 | tf_op jit(solution)/shard_map/all_to_all | solution.py:28
  74.2 31.3 %collective-permute-start.9 = (bf16[320,1280]{1,0:T(8,128)(2,1)}, bf16[320,1280]{1,0:T(8,128)(2,1)}, u32[]{:S(2)}, u32[]{:S(2)}) collective-permute-start(bf16[320,1280]{1,0:T(8,128)(2,1)} %bitcast.12), channel_id=1, source_target_pairs={{0,8},{8,0},{16,24},{24,16},{1,9},{9,1},{17,25},{25,17},{2,10},{10... | collective-permute-start | bytes 2457608 | tf_op jit(solution)/shard_map/ppermute | solution.py:24
  89.3 53.5 %all-to-all-start.5 = ((bf16[8,80,1280]{2,1,0:T(8,128)(2,1)}), bf16[8,80,1280]{2,1,0:T(8,128)(2,1)}, u32[]{:S(2)}, u32[]{:S(2)}) async-start(bf16[8,80,1280]{2,1,0:T(8,128)(2,1)} %bitcast.167), calls=%async_computation.5 | async-start | bytes 3276800 | tf_op jit(solution)/shard_map/all_to_all | solution.py:28
  95.2 52.7 %collective-permute-start.8 = (bf16[320,1280]{1,0:T(8,128)(2,1)}, bf16[320,1280]{1,0:T(8,128)(2,1)}, u32[]{:S(2)}, u32[]{:S(2)}) collective-permute-start(bf16[320,1280]{1,0:T(8,128)(2,1)} %bitcast.9), channel_id=1, source_target_pairs={{0,8},{8,0},{16,24},{24,16},{1,9},{9,1},{17,25},{25,17},{2,10},{10... | collective-permute-start | bytes 2457608 | tf_op jit(solution)/shard_map/ppermute | solution.py:24
  109.6 21.5 %collective-permute-start.15 = (bf16[128,1280]{1,0:T(8,128)(2,1)S(1)}, bf16[128,1280]{1,0:T(8,128)(2,1)S(1)}, u32[]{:S(2)}, u32[]{:S(2)}) collective-permute-start(bf16[128,1280]{1,0:T(8,128)(2,1)S(1)} %fusion.40), channel_id=1, source_target_pairs={{0,24},{8,16},{16,8},{24,0},{1,25},{9,17},{17,9},{25,1},{2,26},{10... | collective-permute-start | bytes 983048 | tf_op jit(solution)/shard_map/ppermute | solution.py:24
  110.1 31.0 %collective-permute-start.14 = (bf16[128,1280]{1,0:T(8,128)(2,1)S(1)}, bf16[128,1280]{1,0:T(8,128)(2,1)S(1)}, u32[]{:S(2)}, u32[]{:S(2)}) collective-permute-start(bf16[128,1280]{1,0:T(8,128)(2,1)S(1)} %fusion.40), channel_id=1, source_target_pairs={{0,16},{8,24},{16,0},{24,8},{1,17},{9,25},{17,1},{25,9},{2,18},{10... | collective-permute-start | bytes 983048 | tf_op jit(solution)/shard_map/ppermute | solution.py:24
  142.8 35.5 %all-to-all-start.4 = ((bf16[8,80,1280]{2,1,0:T(8,128)(2,1)}), bf16[8,80,1280]{2,1,0:T(8,128)(2,1)}, u32[]{:S(2)}, u32[]{:S(2)}) async-start(bf16[8,80,1280]{2,1,0:T(8,128)(2,1)} %bitcast.168), calls=%async_computation.4 | async-start | bytes 3276800 | tf_op jit(solution)/shard_map/all_to_all | solution.py:28
  199.9 12.8 %all-to-all-start.7 = ((f32[8,8,128]{2,1,0:T(8,128)}), f32[8,8,128]{2,1,0:T(8,128)S(1)}, u32[]{:S(2)}, u32[]{:S(2)}) async-start(f32[8,8,128]{2,1,0:T(8,128)} %copy.39), calls=%async_computation.7 | async-start | bytes 65536 | tf_op jit(solution)/shard_map/all_to_all | solution.py:28
  210.7 38.7 %collective-permute-start.13 = (bf16[320,1280]{1,0:T(8,128)(2,1)}, bf16[320,1280]{1,0:T(8,128)(2,1)S(1)}, u32[]{:S(2)}, u32[]{:S(2)}) collective-permute-start(bf16[320,1280]{1,0:T(8,128)(2,1)} %slice.291), channel_id=1, source_target_pairs={{0,8},{8,0},{16,24},{24,16},{1,9},{9,1},{17,25},{25,17},{2,10},{10... | collective-permute-start | bytes 2457608 | tf_op jit(solution)/shard_map/ppermute | solution.py:24
  210.7 77.2 %collective-permute-start.23 = (bf16[320,1280]{1,0:T(8,128)(2,1)}, bf16[320,1280]{1,0:T(8,128)(2,1)}, u32[]{:S(2)}, u32[]{:S(2)}) collective-permute-start(bf16[320,1280]{1,0:T(8,128)(2,1)} %slice.302), channel_id=1, source_target_pairs={{0,8},{8,0},{16,24},{24,16},{1,9},{9,1},{17,25},{25,17},{2,10},{10... | collective-permute-start | bytes 2457608 | tf_op jit(solution)/shard_map/ppermute | solution.py:24
  212.8 38.9 %all-to-all-start.6 = ((bf16[8,80,1280]{2,1,0:T(8,128)(2,1)}), bf16[8,80,1280]{2,1,0:T(8,128)(2,1)}, u32[]{:S(2)}, u32[]{:S(2)}) async-start(bf16[8,80,1280]{2,1,0:T(8,128)(2,1)} %bitcast.166), calls=%async_computation.6 | async-start | bytes 3276800 | tf_op jit(solution)/shard_map/all_to_all | solution.py:28
  221.8 25.3 %collective-permute-start.21 = (f32[2,128]{1,0:T(2,128)}, f32[2,128]{1,0:T(2,128)S(1)}, u32[]{:S(2)}, u32[]{:S(2)}) collective-permute-start(f32[2,128]{1,0:T(2,128)} %get-tuple-element.119), channel_id=1, source_target_pairs={{0,16},{8,24},{16,0},{24,8},{1,17},{9,25},{17,1},{25,9},{2,18},{10... | collective-permute-start | bytes 3080 | tf_op jit(solution)/shard_map/ppermute | solution.py:24
  221.8 26.8 %collective-permute-start.22 = (f32[2,128]{1,0:T(2,128)S(1)}, f32[2,128]{1,0:T(2,128)S(1)}, u32[]{:S(2)}, u32[]{:S(2)}) collective-permute-start(f32[2,128]{1,0:T(2,128)S(1)} %get-tuple-element.120), channel_id=1, source_target_pairs={{0,24},{8,16},{16,8},{24,0},{1,25},{9,17},{17,9},{25,1},{2,26},{10... | collective-permute-start | bytes 3080 | tf_op jit(solution)/shard_map/ppermute | solution.py:24
  224.2 25.1 %collective-permute-start.20 = (f32[2,128]{1,0:T(2,128)S(1)}, f32[2,128]{1,0:T(2,128)S(1)}, u32[]{:S(2)}, u32[]{:S(2)}) collective-permute-start(f32[2,128]{1,0:T(2,128)S(1)} %pad_maximum_fusion.3), channel_id=1, source_target_pairs={{0,8},{8,0},{16,24},{24,16},{1,9},{9,1},{17,25},{25,17},{2,10},{10... | collective-permute-start | bytes 3080 | tf_op jit(solution)/shard_map/ppermute | solution.py:24
  251.7 16.7 %all-to-all-start.3 = ((bf16[8,40,1280]{2,1,0:T(8,128)(2,1)}), bf16[8,40,1280]{2,1,0:T(8,128)(2,1)S(1)}, u32[]{:S(2)}, u32[]{:S(2)}) async-start(bf16[8,40,1280]{2,1,0:T(8,128)(2,1)} %bitcast.160), calls=%async_computation.3 | async-start | bytes 1638400 | tf_op jit(solution)/shard_map/all_to_all | solution.py:28
  258.6 25.1 %collective-permute-start.18 = (bf16[128,1280]{1,0:T(8,128)(2,1)}, bf16[128,1280]{1,0:T(8,128)(2,1)}, u32[]{:S(2)}, u32[]{:S(2)}) collective-permute-start(bf16[128,1280]{1,0:T(8,128)(2,1)} %get-tuple-element.95), channel_id=1, source_target_pairs={{0,16},{8,24},{16,0},{24,8},{1,17},{9,25},{17,1},{25,9},{2,18},{10... | collective-permute-start | bytes 983048 | tf_op jit(solution)/shard_map/ppermute | solution.py:24
  259.7 24.0 %collective-permute-start.19 = (bf16[128,1280]{1,0:T(8,128)(2,1)}, bf16[128,1280]{1,0:T(8,128)(2,1)}, u32[]{:S(2)}, u32[]{:S(2)}) collective-permute-start(bf16[128,1280]{1,0:T(8,128)(2,1)} %get-tuple-element.96), channel_id=1, source_target_pairs={{0,24},{8,16},{16,8},{24,0},{1,25},{9,17},{17,9},{25,1},{2,26},{10... | collective-permute-start | bytes 983048 | tf_op jit(solution)/shard_map/ppermute | solution.py:24
  268.4 26.1 %all-to-all-start.9 = ((bf16[8,80,1280]{2,1,0:T(8,128)(2,1)}), bf16[8,80,1280]{2,1,0:T(8,128)(2,1)}, u32[]{:S(2)}, u32[]{:S(2)}) async-start(bf16[8,80,1280]{2,1,0:T(8,128)(2,1)} %bitcast.165), calls=%async_computation.9 | async-start | bytes 3276800 | tf_op jit(solution)/shard_map/all_to_all | solution.py:28
  286.0 65.9 %copy-start.2 = (bf16[128,1280]{1,0:T(8,128)(2,1)}, bf16[128,1280]{1,0:T(8,128)(2,1)S(1)}, u32[]{:S(2)}) copy-start(bf16[128,1280]{1,0:T(8,128)(2,1)S(1)} %add_convert_fusion.3) | copy-start | bytes 983044
  287.9 43.3 %collective-permute-start.26 = (bf16[640,1408]{1,0:T(8,128)(2,1)}, bf16[640,1408]{1,0:T(8,128)(2,1)}, u32[]{:S(2)}, u32[]{:S(2)}) collective-permute-start(bf16[640,1408]{1,0:T(8,128)(2,1)} %pad_maximum_fusion), channel_id=1, source_target_pairs={{0,1},{1,0},{2,3},{3,2},{4,5},{5,4},{6,7},{7,6},{8,9},{9,8},{10,11... | collective-permute-start | bytes 5406728 | tf_op jit(solution)/shard_map/ppermute | solution.py:24
  294.5 24.6 %all-to-all-start.8 = ((bf16[8,40,1280]{2,1,0:T(8,128)(2,1)}), bf16[8,40,1280]{2,1,0:T(8,128)(2,1)S(1)}, u32[]{:S(2)}, u32[]{:S(2)}) async-start(bf16[8,40,1280]{2,1,0:T(8,128)(2,1)} %bitcast.159), calls=%async_computation.8 | async-start | bytes 1638400 | tf_op jit(solution)/shard_map/all_to_all | solution.py:28
  301.1 28.0 %collective-permute-start.24 = (bf16[128,1280]{1,0:T(8,128)(2,1)}, bf16[128,1280]{1,0:T(8,128)(2,1)}, u32[]{:S(2)}, u32[]{:S(2)}) collective-permute-start(bf16[128,1280]{1,0:T(8,128)(2,1)} %get-tuple-element.93), channel_id=1, source_target_pairs={{0,16},{8,24},{16,0},{24,8},{1,17},{9,25},{17,1},{25,9},{2,18},{10... | collective-permute-start | bytes 983048 | tf_op jit(solution)/shard_map/ppermute | solution.py:24
  306.1 22.9 %collective-permute-start.25 = (bf16[128,1280]{1,0:T(8,128)(2,1)}, bf16[128,1280]{1,0:T(8,128)(2,1)}, u32[]{:S(2)}, u32[]{:S(2)}) collective-permute-start(bf16[128,1280]{1,0:T(8,128)(2,1)} %get-tuple-element.94), channel_id=1, source_target_pairs={{0,24},{8,16},{16,8},{24,0},{1,25},{9,17},{17,9},{25,1},{2,26},{10... | collective-permute-start | bytes 983048 | tf_op jit(solution)/shard_map/ppermute | solution.py:24
  335.4 11.2 %collective-permute-start.27 = (bf16[320,640]{1,0:T(8,128)(2,1)S(1)}, bf16[320,640]{1,0:T(8,128)(2,1)S(1)}, u32[]{:S(2)}, u32[]{:S(2)}) collective-permute-start(bf16[320,640]{1,0:T(8,128)(2,1)S(1)} %concatenate.148), channel_id=1, source_target_pairs={{0,2},{1,3},{2,0},{3,1},{4,6},{5,7},{6,4},{7,5},{8,10},{9,11},{10,... | collective-permute-start | bytes 1228808 | tf_op jit(solution)/shard_map/ppermute | solution.py:24
  337.5 13.1 %collective-permute-start.29 = (bf16[320,768]{1,0:T(8,128)(2,1)S(1)}, bf16[320,768]{1,0:T(8,128)(2,1)S(1)}, u32[]{:S(2)}, u32[]{:S(2)}) collective-permute-start(bf16[320,768]{1,0:T(8,128)(2,1)S(1)} %maximum_maximum_fusion), channel_id=1, source_target_pairs={{0,4},{1,5},{2,6},{3,7},{4,0},{5,1},{6,2},{7,3},{8,12},{9,13},{10,... | collective-permute-start | bytes 1474568 | tf_op jit(solution)/shard_map/ppermute | solution.py:24
  346.6 7.3 %collective-permute-start.28 = (bf16[160,640]{1,0:T(8,128)(2,1)S(1)}, bf16[160,640]{1,0:T(8,128)(2,1)S(1)}, u32[]{:S(2)}, u32[]{:S(2)}) collective-permute-start(bf16[160,640]{1,0:T(8,128)(2,1)S(1)} %get-tuple-element.90), channel_id=1, source_target_pairs={{0,4},{1,5},{2,6},{3,7},{4,0},{5,1},{6,2},{7,3},{8,12},{9,13},{10,... | collective-permute-start | bytes 614408 | tf_op jit(solution)/shard_map/ppermute | solution.py:24
  350.7 6.3 %collective-permute-start.30 = (bf16[160,768]{1,0:T(8,128)(2,1)S(1)}, bf16[160,768]{1,0:T(8,128)(2,1)S(1)}, u32[]{:S(2)}, u32[]{:S(2)}) collective-permute-start(bf16[160,768]{1,0:T(8,128)(2,1)S(1)} %fusion.41), channel_id=1, source_target_pairs={{0,2},{1,3},{2,0},{3,1},{4,6},{5,7},{6,4},{7,5},{8,10},{9,11},{10,... | collective-permute-start | bytes 737288 | tf_op jit(solution)/shard_map/ppermute | solution.py:24
  357.3 11.2 %collective-permute-start.31 = (bf16[40,1408]{1,0:T(8,128)(2,1)S(1)}, bf16[40,1408]{1,0:T(8,128)(2,1)S(1)}, u32[]{:S(2)}, u32[]{:S(2)}) collective-permute-start(bf16[40,1408]{1,0:T(8,128)(2,1)S(1)} %get-tuple-element.97), channel_id=1, source_target_pairs={{0,8},{8,0},{16,24},{24,16},{1,9},{9,1},{17,25},{25,17},{2,10},{10... | collective-permute-start | bytes 337928 | tf_op jit(solution)/shard_map/ppermute | solution.py:24
  364.7 6.7 %collective-permute-start.33 = (bf16[40,1408]{1,0:T(8,128)(2,1)S(1)}, bf16[40,1408]{1,0:T(8,128)(2,1)S(1)}, u32[]{:S(2)}, u32[]{:S(2)}) collective-permute-start(bf16[40,1408]{1,0:T(8,128)(2,1)S(1)} %get-tuple-element.98), channel_id=1, source_target_pairs={{0,24},{8,16},{16,8},{24,0},{1,25},{9,17},{17,9},{25,1},{2,26},{10... | collective-permute-start | bytes 337928 | tf_op jit(solution)/shard_map/ppermute | solution.py:24
  366.3 7.5 %collective-permute-start.32 = (bf16[40,1408]{1,0:T(8,128)(2,1)S(1)}, bf16[40,1408]{1,0:T(8,128)(2,1)S(1)}, u32[]{:S(2)}, u32[]{:S(2)}) collective-permute-start(bf16[40,1408]{1,0:T(8,128)(2,1)S(1)} %get-tuple-element.99), channel_id=1, source_target_pairs={{0,16},{8,24},{16,0},{24,8},{1,17},{9,25},{17,1},{25,9},{2,18},{10... | collective-permute-start | bytes 337928 | tf_op jit(solution)/shard_map/ppermute | solution.py:24
  (21 other events, 126.9 us)
